TPU v7x, 32 devices: a whole 2x2x4 slice. The times are simulated.
32 devices in a mesh: section: 2 (over y), dp: 16 (over z, x, core).
Axes of the slice: x: 2, y: 2, z: 4, core: 2. Of those that a mesh axis runs over, the one named last changes fastest.
Arguments:
- mel_input: bfloat16 [32, 80, 2048], P('dp'), may hold values from -6 to 6
- time_start: int32 [32], P('dp'), may hold values from 0 to 2047
- time_width: int32 [32], P('dp'), may hold values from 0 to 100
- freq_start: int32 [32], P('dp'), may hold values from 0 to 79
- freq_width: int32 [32], P('dp'), may hold values from 0 to 27
- text_len: int32 [32], P('dp'), may hold values from 5 to 448, as said below
- text_embed: bfloat16 [32, 448, 512], P('dp'), may hold values from -6 to 6
- cotangent: bfloat16 [32, 448, 512], P('dp'), may hold values from -6 to 6
- positions: bfloat16 [1024, 512], replicated, may hold values from -1 to 1
- conv_first: bfloat16 [3, 80, 512], P(None, None, 'section'), may hold values from -0.375 to 0.375
- conv_first_bias: bfloat16 [512], P('section'), may hold values from -3 to 3
- conv_second: bfloat16 [3, 512, 512], P(None, None, 'section'), may hold values from -0.15625 to 0.15625
- norm_gain: bfloat16 [2, 3, 512], P('section'), may hold values from 0.5 to 1.5
- norm_shift: bfloat16 [2, 3, 512], P('section'), may hold values from -1.5 to 1.5
- attn_in: bfloat16 [2, 512, 1536], P('section'), may hold values from -0.25 to 0.25
- attn_out: bfloat16 [2, 512, 512], P('section'), may hold values from -1.5 to 1.5
- mlp_up: bfloat16 [2, 512, 2048], P('section'), may hold values from -0.25 to 0.25
- mlp_down: bfloat16 [2, 2048, 512], P('section'), may hold values from -0.125 to 0.125
- up_bias: bfloat16 [2, 2048], P('section'), may hold values from -1 to 1
- small_bias: bfloat16 [2, 6, 512], P('section'), may hold values from -0.5 to 0.5
- cross_first: bfloat16 [2, 512, 512], P('section'), may hold values from -0.25 to 0.25
- cross_second: bfloat16 [2, 512, 512], P('section'), may hold values from -1 to 1
Outputs:
- decoded: float32 [32, 448, 512], P('dp', None, 'section')
- text_grad: float32 [32, 448, 512], P('dp', None, 'section')
- mel_grad: float32 [32, 80, 2048], P('dp', None, 'section')
- conv_first_grad: float32 [3, 80, 512], P(None, None, 'section')
- conv_first_bias_grad: float32 [512], P('section')
- conv_second_grad: float32 [3, 512, 512], P(None, None, 'section')
- norm_gain_grad: float32 [2, 3, 512], P('section')
- norm_shift_grad: float32 [2, 3, 512], P('section')
- attn_in_grad: float32 [2, 512, 1536], P('section')
- attn_out_grad: float32 [2, 512, 512], P('section')
- mlp_up_grad: float32 [2, 512, 2048], P('section')
- mlp_down_grad: float32 [2, 2048, 512], P('section')
- up_bias_grad: float32 [2, 2048], P('section')
- small_bias_grad: float32 [2, 6, 512], P('section')
- cross_first_grad: float32 [2, 512, 512], P('section')
- cross_second_grad: float32 [2, 512, 512], P('section')
- cross_bias_grad: float32 [512], P('section')
Inputs may be any that keep to these rules, and one draw needn't show every extreme that they name: `text_len`: in every draw some clip has exactly 448 text positions and some exactly 5.
All inputs are finite; a program needn't handle non-finite values.
Results may differ from a plain program's by a relative error of at most 0.025.
Values may be sent and summed in bfloat16 or wider, within the bound.
A program may use at most 384 MiB of HBM per device.

v0:
```python
import jax
import jax.numpy as jnp
from jax import lax
from jax.sharding import PartitionSpec as P

HEADS = 8


epsilon = 1e-05
root_half = 0.7071067811865476
gauss_norm = 0.3989422804014327


def shifted(shard, axis, by):
    size = lax.axis_size(axis)
    pairs = [(i, i + by) for i in range(size) if 0 <= i + by < size]
    return lax.ppermute(shard, axis, pairs)


def gelu_value(inputs):
    return 0.5 * inputs * (1.0 + lax.erf(inputs * root_half))


def gelu_slope(inputs):
    return 0.5 * (1.0 + lax.erf(inputs * root_half)) + inputs * gauss_norm * jnp.exp(
        -0.5 * inputs * inputs
    )


def matmul(left, right):
    return jnp.dot(left, right, preferred_element_type=jnp.float32)


def weight_grad(inputs, grad_low):
    return lax.dot_general(
        inputs, grad_low, (((0,), (0,)), ((), ())), preferred_element_type=jnp.float32
    )


def input_grad(grad_low, weight):
    return lax.dot_general(
        grad_low, weight, (((1,), (1,)), ((), ())), preferred_element_type=jnp.float32
    )


def norm_rows(inputs, gain, shift):
    centred = inputs - jnp.mean(inputs, axis=-1, keepdims=True)
    inverse = lax.rsqrt(jnp.mean(centred * centred, axis=-1, keepdims=True) + epsilon)
    normed = centred * inverse
    return (normed * gain.astype(jnp.float32) + shift.astype(jnp.float32), normed, inverse)


def norm_rows_back(grad, gain, normed, inverse):
    scaled = grad * gain.astype(jnp.float32)
    grad_inputs = inverse * (
        scaled
        - jnp.mean(scaled, axis=-1, keepdims=True)
        - normed * jnp.mean(scaled * normed, axis=-1, keepdims=True)
    )
    return (grad_inputs, jnp.sum(grad * normed, axis=0), jnp.sum(grad, axis=0))


def spec_keep(time_begin, time_span, band_begin, band_span, band_count, frame_count):
    frame_at = jnp.arange(frame_count, dtype=jnp.int32)
    band_at = jnp.arange(band_count, dtype=jnp.int32)
    keep_time = jnp.logical_or(frame_at < time_begin, frame_at >= time_begin + time_span)
    keep_band = jnp.logical_or(band_at < band_begin, band_at >= band_begin + band_span)
    return jnp.logical_and(keep_band[:, None], keep_time[None, :])


def conv_tap(padded, weight, tap_index, frame_count):
    return jnp.einsum(
        "mt,mc->tc",
        padded[:, tap_index : tap_index + frame_count],
        weight[tap_index],
        preferred_element_type=jnp.float32,
    )


def stem_first(masked, weight, bias):
    frame_count = masked.shape[1]
    padded = jnp.pad(masked, ((0, 0), (1, 1)))
    conv_sum = (
        conv_tap(padded, weight, 0, frame_count)
        + conv_tap(padded, weight, 1, frame_count)
        + conv_tap(padded, weight, 2, frame_count)
    )
    pre_act = conv_sum + bias.astype(jnp.float32)
    return (pre_act, gelu_value(pre_act).astype(jnp.bfloat16))


def stem_first_back(masked, weight, pre_act, grad_hidden):
    frame_count = masked.shape[1]
    padded = jnp.pad(masked, ((0, 0), (1, 1)))
    grad_pre = grad_hidden * gelu_slope(pre_act)
    grad_low = grad_pre.astype(jnp.bfloat16)
    grad_weight = jnp.stack(
        [
            jnp.einsum(
                "mt,tc->mc",
                padded[:, tap_index : tap_index + frame_count],
                grad_low,
                preferred_element_type=jnp.float32,
            )
            for tap_index in range(3)
        ]
    )
    parts = [
        jnp.einsum("tc,mc->mt", grad_low, weight[tap_index], preferred_element_type=jnp.float32)
        for tap_index in range(3)
    ]
    grad_masked = (
        parts[1]
        + jnp.pad(parts[0][:, 1:], ((0, 0), (0, 1)))
        + jnp.pad(parts[2][:, :-1], ((0, 0), (1, 0)))
    )
    return (grad_weight, jnp.sum(grad_pre, axis=0), grad_masked)


def odd_even(hidden):
    pairs = hidden.reshape(hidden.shape[0] // 2, 2, hidden.shape[1])
    even_rows = pairs[:, 0]
    odd_rows = pairs[:, 1]
    prior_rows = jnp.pad(odd_rows, ((1, 0), (0, 0)))[:-1]
    return (prior_rows, even_rows, odd_rows)


def stem_second(hidden, weight):
    prior_rows, even_rows, odd_rows = odd_even(hidden)
    return (
        matmul(prior_rows, weight[0]) + matmul(even_rows, weight[1]) + matmul(odd_rows, weight[2])
    )


def stem_second_back(hidden, weight, grad_low):
    prior_rows, even_rows, odd_rows = odd_even(hidden)
    grad_weight = jnp.stack(
        [
            weight_grad(prior_rows, grad_low),
            weight_grad(even_rows, grad_low),
            weight_grad(odd_rows, grad_low),
        ]
    )
    grad_prior = input_grad(grad_low, weight[0])
    grad_even = input_grad(grad_low, weight[1])
    grad_odd = input_grad(grad_low, weight[2]) + jnp.pad(grad_prior[1:], ((0, 1), (0, 0)))
    grad_hidden = jnp.stack([grad_even, grad_odd], axis=1).reshape(hidden.shape[0], -1)
    return (grad_weight, grad_hidden)


def head_split(inputs):
    return inputs.reshape(inputs.shape[0], HEADS, inputs.shape[1] // HEADS)


def block_scores(query_block, key_heads, block_start, causal):
    score_scale = float(key_heads.shape[2]) ** (-0.5)
    scores = (
        jnp.einsum("qhd,khd->hqk", query_block, key_heads, preferred_element_type=jnp.float32)
        * score_scale
    )
    if causal:
        rows_at = block_start + jnp.arange(query_block.shape[0], dtype=jnp.int32)
        keys_at = jnp.arange(key_heads.shape[0], dtype=jnp.int32)
        scores = jnp.where(keys_at[None, None, :] <= rows_at[None, :, None], scores, -1e30)
    return scores


def attend(queries, memory_keys, memory_values, causal):
    row_count = queries.shape[0]
    block_rows = min(row_count, 512)
    block_count = row_count // block_rows
    key_heads = head_split(memory_keys)
    value_heads = head_split(memory_values)
    query_blocks = queries.reshape(block_count, block_rows, HEADS, -1)
    block_starts = jnp.arange(block_count, dtype=jnp.int32) * block_rows

    def one_block(block_item):
        query_block, block_start = block_item
        scores = block_scores(query_block, key_heads, block_start, causal)
        row_max = jnp.max(scores, axis=-1, keepdims=True)
        exponent = jnp.exp(scores - row_max)
        row_total = jnp.sum(exponent, axis=-1, keepdims=True)
        probability = (exponent / row_total).astype(jnp.bfloat16)
        mixed_heads = jnp.einsum(
            "hqk,khd->qhd", probability, value_heads, preferred_element_type=jnp.float32
        )
        return (
            mixed_heads.reshape(block_rows, -1).astype(jnp.bfloat16),
            (row_max + jnp.log(row_total))[..., 0],
        )

    mixed_heads, log_total = lax.map(one_block, (query_blocks, block_starts))
    return (mixed_heads.reshape(row_count, -1), log_total)


def attend_back(queries, memory_keys, memory_values, log_total, grad_mixed, causal):
    row_count = queries.shape[0]
    block_rows = min(row_count, 512)
    block_count = row_count // block_rows
    score_scale = float(queries.shape[1] // HEADS) ** (-0.5)
    key_heads = head_split(memory_keys)
    value_heads = head_split(memory_values)
    query_blocks = queries.reshape(block_count, block_rows, HEADS, -1)
    grad_blocks = grad_mixed.reshape(block_count, block_rows, HEADS, -1)
    block_starts = jnp.arange(block_count, dtype=jnp.int32) * block_rows

    def one_block(running, block_item):
        grad_keys, grad_values = running
        query_block, grad_block, total_block, block_start = block_item
        probability = jnp.exp(
            block_scores(query_block, key_heads, block_start, causal) - total_block[..., None]
        )
        grad_prob = jnp.einsum(
            "qhd,khd->hqk", grad_block, value_heads, preferred_element_type=jnp.float32
        )
        grad_values = grad_values + jnp.einsum(
            "hqk,qhd->khd",
            probability.astype(jnp.bfloat16),
            grad_block,
            preferred_element_type=jnp.float32,
        )
        grad_scores = (
            probability * (grad_prob - jnp.sum(probability * grad_prob, axis=-1, keepdims=True))
        ).astype(jnp.bfloat16)
        grad_query = (
            jnp.einsum("hqk,khd->qhd", grad_scores, key_heads, preferred_element_type=jnp.float32)
            * score_scale
        )
        grad_keys = (
            grad_keys
            + jnp.einsum(
                "hqk,qhd->khd", grad_scores, query_block, preferred_element_type=jnp.float32
            )
            * score_scale
        )
        return ((grad_keys, grad_values), grad_query.reshape(block_rows, -1))

    zero_keys = jnp.zeros(key_heads.shape, jnp.float32)
    (grad_keys, grad_values), grad_queries = lax.scan(
        one_block, (zero_keys, zero_keys), (query_blocks, grad_blocks, log_total, block_starts)
    )
    key_count = memory_keys.shape[0]
    return (
        grad_queries.reshape(row_count, -1),
        grad_keys.reshape(key_count, -1),
        grad_values.reshape(key_count, -1),
    )


def self_block(
    inputs, gain, shift, weight_in, weight_out, bias_query, bias_value, bias_out, causal
):
    model_width = inputs.shape[1]
    normed_in, normed, inverse = norm_rows(inputs, gain, shift)
    normed_low = normed_in.astype(jnp.bfloat16)
    joint = matmul(normed_low, weight_in)
    queries = (joint[:, :model_width] + bias_query.astype(jnp.float32)).astype(jnp.bfloat16)
    memory_keys = joint[:, model_width : 2 * model_width].astype(jnp.bfloat16)
    memory_values = (joint[:, 2 * model_width :] + bias_value.astype(jnp.float32)).astype(
        jnp.bfloat16
    )
    mixed_heads, log_total = attend(queries, memory_keys, memory_values, causal)
    result = inputs + matmul(mixed_heads, weight_out) + bias_out.astype(jnp.float32)
    return (
        result,
        (normed, inverse, normed_low, queries, memory_keys, memory_values, mixed_heads, log_total),
    )


def self_block_back(grad, kept, gain, weight_in, weight_out, causal):
    normed, inverse, normed_low, queries, memory_keys, memory_values, mixed_heads, log_total = kept
    grad_low = grad.astype(jnp.bfloat16)
    grad_weight_out = weight_grad(mixed_heads, grad_low)
    grad_mixed = input_grad(grad_low, weight_out).astype(jnp.bfloat16)
    grad_query, grad_key, grad_value = attend_back(
        queries, memory_keys, memory_values, log_total, grad_mixed, causal
    )
    joint_low = jnp.concatenate([grad_query, grad_key, grad_value], axis=1).astype(jnp.bfloat16)
    grad_weight_in = weight_grad(normed_low, joint_low)
    grad_normed = input_grad(joint_low, weight_in)
    grad_inputs, grad_gain, grad_shift = norm_rows_back(grad_normed, gain, normed, inverse)
    return (
        grad + grad_inputs,
        (
            grad_gain,
            grad_shift,
            grad_weight_in,
            grad_weight_out,
            jnp.sum(grad_query, axis=0),
            jnp.sum(grad_value, axis=0),
            jnp.sum(grad, axis=0),
        ),
    )


def feed_block(inputs, gain, shift, weight_up, bias_up, weight_down, bias_down):
    normed_in, normed, inverse = norm_rows(inputs, gain, shift)
    normed_low = normed_in.astype(jnp.bfloat16)
    hidden_pre = matmul(normed_low, weight_up) + bias_up.astype(jnp.float32)
    hidden = gelu_value(hidden_pre).astype(jnp.bfloat16)
    result = inputs + matmul(hidden, weight_down) + bias_down.astype(jnp.float32)
    return (result, (normed, inverse, normed_low, hidden_pre, hidden))


def feed_block_back(grad, kept, gain, weight_up, weight_down):
    normed, inverse, normed_low, hidden_pre, hidden = kept
    grad_low = grad.astype(jnp.bfloat16)
    grad_weight_down = weight_grad(hidden, grad_low)
    grad_pre = input_grad(grad_low, weight_down) * gelu_slope(hidden_pre)
    pre_low = grad_pre.astype(jnp.bfloat16)
    grad_weight_up = weight_grad(normed_low, pre_low)
    grad_normed = input_grad(pre_low, weight_up)
    grad_inputs, grad_gain, grad_shift = norm_rows_back(grad_normed, gain, normed, inverse)
    return (
        grad + grad_inputs,
        (
            grad_gain,
            grad_shift,
            grad_weight_up,
            grad_weight_down,
            jnp.sum(grad_pre, axis=0),
            jnp.sum(grad, axis=0),
        ),
    )


def encode(conv_out, positions, weights):
    (
        gains,
        shifts,
        weight_in,
        weight_out,
        weight_up,
        weight_down,
        bias_up,
        small,
        cross_a,
        cross_b,
    ) = weights
    second_pre = conv_out + small[4].astype(jnp.float32)
    encoded = gelu_value(second_pre) + positions.astype(jnp.float32)
    middle, kept_attn = self_block(
        encoded, gains[0], shifts[0], weight_in, weight_out, small[0], small[1], small[2], False
    )
    ending, kept_feed = feed_block(
        middle, gains[1], shifts[1], weight_up, bias_up, weight_down, small[3]
    )
    memory_in, normed, inverse = norm_rows(ending, gains[2], shifts[2])
    memory = memory_in.astype(jnp.bfloat16)
    memory_keys = matmul(memory, cross_a).astype(jnp.bfloat16)
    memory_values = (matmul(memory, cross_b) + small[5].astype(jnp.float32)).astype(jnp.bfloat16)
    return (memory_keys, memory_values, (second_pre, kept_attn, kept_feed, normed, inverse, memory))


def blank_encode(frame_count, model_width, hidden_width):
    block_rows = min(frame_count, 512)
    block_count = frame_count // block_rows
    wide_f32 = jnp.zeros((frame_count, model_width), jnp.float32)
    wide_low = jnp.zeros((frame_count, model_width), jnp.bfloat16)
    column = jnp.zeros((frame_count, 1), jnp.float32)
    log_blank = jnp.zeros((block_count, HEADS, block_rows), jnp.float32)
    kept_attn = (wide_f32, column, wide_low, wide_low, wide_low, wide_low, wide_low, log_blank)
    kept_feed = (
        wide_f32,
        column,
        wide_low,
        jnp.zeros((frame_count, hidden_width), jnp.float32),
        jnp.zeros((frame_count, hidden_width), jnp.bfloat16),
    )
    return (wide_low, wide_low, (wide_f32, kept_attn, kept_feed, wide_f32, column, wide_low))


def encode_back(keys_back, values_back, kept, weights):
    (
        gains,
        shifts,
        weight_in,
        weight_out,
        weight_up,
        weight_down,
        bias_up,
        small,
        cross_a,
        cross_b,
    ) = weights
    second_pre, kept_attn, kept_feed, normed, inverse, memory = kept
    grad_cross_a = weight_grad(memory, keys_back)
    grad_cross_b = weight_grad(memory, values_back)
    grad_memory = input_grad(keys_back, cross_a) + input_grad(values_back, cross_b)
    grad_ending, gain_post, shift_post = norm_rows_back(grad_memory, gains[2], normed, inverse)
    grad_middle, feed_grads = feed_block_back(
        grad_ending, kept_feed, gains[1], weight_up, weight_down
    )
    grad_encoded, attn_grads = self_block_back(
        grad_middle, kept_attn, gains[0], weight_in, weight_out, False
    )
    grad_second = grad_encoded * gelu_slope(second_pre)
    grad_gains = jnp.stack([attn_grads[0], feed_grads[0], gain_post])
    grad_shifts = jnp.stack([attn_grads[1], feed_grads[1], shift_post])
    grad_small = jnp.stack(
        [
            attn_grads[4],
            attn_grads[5],
            attn_grads[6],
            feed_grads[5],
            jnp.sum(grad_second, axis=0),
            jnp.sum(values_back.astype(jnp.float32), axis=0),
        ]
    )
    grads = (
        grad_gains,
        grad_shifts,
        attn_grads[2],
        attn_grads[3],
        feed_grads[2],
        feed_grads[3],
        feed_grads[4],
        grad_small,
        grad_cross_a,
        grad_cross_b,
    )
    return (grads, grad_second)


def decode(text_clip, cot_clip, text_length, memory_keys, memory_values, weights):
    (
        gains,
        shifts,
        weight_in,
        weight_out,
        weight_up,
        weight_down,
        bias_up,
        small,
        cross_a,
        cross_b,
    ) = weights
    middle, kept_attn = self_block(
        text_clip.astype(jnp.float32),
        gains[0],
        shifts[0],
        weight_in,
        weight_out,
        small[0],
        small[1],
        small[2],
        True,
    )
    cross_in, cross_normed, cross_inverse = norm_rows(middle, gains[1], shifts[1])
    cross_low = cross_in.astype(jnp.bfloat16)
    queries = (matmul(cross_low, cross_a) + small[4].astype(jnp.float32)).astype(jnp.bfloat16)
    mixed_heads, log_total = attend(queries, memory_keys, memory_values, False)
    after = middle + matmul(mixed_heads, cross_b) + small[5].astype(jnp.float32)
    ending, kept_feed = feed_block(
        after, gains[2], shifts[2], weight_up, bias_up, weight_down, small[3]
    )
    valid = (jnp.arange(text_clip.shape[0], dtype=jnp.int32) < text_length)[:, None]
    decoded = jnp.where(valid, ending, 0.0)
    grad_ending = jnp.where(valid, cot_clip.astype(jnp.float32), 0.0)
    grad_after, feed_grads = feed_block_back(
        grad_ending, kept_feed, gains[2], weight_up, weight_down
    )
    after_low = grad_after.astype(jnp.bfloat16)
    grad_cross_b = weight_grad(mixed_heads, after_low)
    grad_mixed = input_grad(after_low, cross_b).astype(jnp.bfloat16)
    grad_query, grad_key, grad_value = attend_back(
        queries, memory_keys, memory_values, log_total, grad_mixed, False
    )
    query_low = grad_query.astype(jnp.bfloat16)
    grad_cross_a = weight_grad(cross_low, query_low)
    grad_cross_in = input_grad(query_low, cross_a)
    grad_cross_x, gain_cross, shift_cross = norm_rows_back(
        grad_cross_in, gains[1], cross_normed, cross_inverse
    )
    grad_text, attn_grads = self_block_back(
        grad_after + grad_cross_x, kept_attn, gains[0], weight_in, weight_out, True
    )
    grad_gains = jnp.stack([attn_grads[0], gain_cross, feed_grads[0]])
    grad_shifts = jnp.stack([attn_grads[1], shift_cross, feed_grads[1]])
    grad_small = jnp.stack(
        [
            attn_grads[4],
            attn_grads[5],
            attn_grads[6],
            feed_grads[5],
            jnp.sum(grad_query, axis=0),
            jnp.sum(grad_after, axis=0),
        ]
    )
    grads = (
        grad_gains,
        grad_shifts,
        attn_grads[2],
        attn_grads[3],
        feed_grads[2],
        feed_grads[3],
        feed_grads[4],
        grad_small,
        grad_cross_a,
        grad_cross_b,
    )
    return (
        decoded,
        grad_text,
        grad_key.astype(jnp.bfloat16),
        grad_value.astype(jnp.bfloat16),
        grads,
    )


def shards(
    mel_input,
    time_start,
    time_width,
    freq_start,
    freq_width,
    text_len,
    text_embed,
    cotangent,
    positions,
    conv_first,
    conv_first_bias,
    conv_second,
    norm_gain,
    norm_shift,
    attn_in,
    attn_out,
    mlp_up,
    mlp_down,
    up_bias,
    small_bias,
    cross_first,
    cross_second,
):
    is_first = lax.axis_index("section") == 0
    weights = (
        norm_gain[0],
        norm_shift[0],
        attn_in[0],
        attn_out[0],
        mlp_up[0],
        mlp_down[0],
        up_bias[0],
        small_bias[0],
        cross_first[0],
        cross_second[0],
    )
    frame_count = positions.shape[0]
    model_width = positions.shape[1]
    hidden_width = mlp_up.shape[2]
    band_count = mel_input.shape[1]
    mel_frames = mel_input.shape[2]
    text_rows = text_embed.shape[1]
    blank_memory = jnp.zeros((frame_count, model_width), jnp.bfloat16)
    blank_text = jnp.zeros((text_rows, model_width), jnp.float32)
    blank_grads = tuple((jnp.zeros(weight.shape, jnp.float32) for weight in weights))
    first_all, bias_all, second_all = (
        lax.all_gather(conv_first, "section", axis=2, tiled=True),
        lax.all_gather(conv_first_bias, "section", axis=0, tiled=True),
        lax.all_gather(conv_second, "section", axis=2, tiled=True),
    )
    stem_shapes = (first_all.shape, bias_all.shape, second_all.shape)
    blank_mel = jnp.zeros((band_count, mel_frames), jnp.float32)
    blank_stem = tuple((jnp.zeros(shape_now, jnp.float32) for shape_now in stem_shapes))

    def clip_step(running, item):
        layer_totals, stem_totals = running
        mel_clip, time_begin, time_span, band_begin, band_span, text_length, text_clip, cot_clip = (
            item
        )
        keep = spec_keep(time_begin, time_span, band_begin, band_span, band_count, mel_frames)
        masked = jnp.where(keep, mel_clip, jnp.zeros_like(mel_clip))

        def forward_first():
            pre_act, hidden = stem_first(masked, first_all, bias_all)
            conv_out = stem_second(hidden, second_all)
            memory_keys, memory_values, kept = encode(conv_out, positions, weights)
            return (memory_keys, memory_values, (pre_act, hidden, kept))

        def forward_blank():
            blank_keys, blank_values, blank_kept = blank_encode(
                frame_count, model_width, hidden_width
            )
            stem_pre = jnp.zeros((mel_frames, model_width), jnp.float32)
            stem_hidden = jnp.zeros((mel_frames, model_width), jnp.bfloat16)
            return (blank_keys, blank_values, (stem_pre, stem_hidden, blank_kept))

        memory_keys, memory_values, saved = lax.cond(is_first, forward_first, forward_blank)
        keys_in, values_in = shifted((memory_keys, memory_values), "section", 1)

        def second_section():
            return decode(text_clip, cot_clip, text_length, keys_in, values_in, weights)

        def second_blank():
            return (blank_text, blank_text, blank_memory, blank_memory, blank_grads)

        decoded, text_grad, grad_keys, grad_values, second_grads = lax.cond(
            is_first, second_blank, second_section
        )
        keys_back, values_back = shifted((grad_keys, grad_values), "section", -1)

        def first_back():
            pre_act, hidden, kept = saved
            first_grads, grad_second = encode_back(keys_back, values_back, kept, weights)
            second_low = grad_second.astype(jnp.bfloat16)
            grad_conv_second, grad_hidden = stem_second_back(hidden, second_all, second_low)
            grad_conv_first, grad_conv_bias, grad_masked = stem_first_back(
                masked, first_all, pre_act, grad_hidden
            )
            return (
                first_grads,
                (grad_conv_first, grad_conv_bias, grad_conv_second),
                jnp.where(keep, grad_masked, 0.0),
            )

        first_grads, stem_grads, mel_grad = lax.cond(
            is_first, first_back, lambda: (blank_grads, blank_stem, blank_mel)
        )
        layer_totals = jax.tree.map(
            lambda total_now, first_now, second_now: total_now + first_now + second_now,
            layer_totals,
            first_grads,
            second_grads,
        )
        stem_totals = jax.tree.map(jnp.add, stem_totals, stem_grads)
        return ((layer_totals, stem_totals), (decoded, text_grad, mel_grad))

    (layer_totals, stem_totals), (decoded_all, text_all, mel_all) = lax.scan(
        clip_step,
        (blank_grads, blank_stem),
        (
            mel_input,
            time_start,
            time_width,
            freq_start,
            freq_width,
            text_len,
            text_embed,
            cotangent,
        ),
    )
    summed = lax.psum(
        (
            layer_totals[0],
            layer_totals[1],
            layer_totals[2],
            layer_totals[3],
            layer_totals[4],
            layer_totals[5],
            layer_totals[6],
            layer_totals[7],
            layer_totals[8],
            layer_totals[9],
            stem_totals[0],
            stem_totals[1],
            stem_totals[2],
        ),
        "dp",
    )
    channel_half = model_width // 2
    moved_first, moved_bias, moved_second = (
        shifted(summed[10][..., channel_half:].astype(jnp.bfloat16), "section", 1).astype(
            jnp.float32
        ),
        shifted(summed[11][channel_half:].astype(jnp.bfloat16), "section", 1).astype(jnp.float32),
        shifted(summed[12][..., channel_half:].astype(jnp.bfloat16), "section", 1).astype(
            jnp.float32
        ),
    )
    conv_first_grad = jnp.where(is_first, summed[10][..., :channel_half], moved_first)
    conv_bias_grad = jnp.where(is_first, summed[11][:channel_half], moved_bias)
    conv_second_grad = jnp.where(is_first, summed[12][..., :channel_half], moved_second)
    frame_half = mel_frames // 2
    mel_moved = shifted(mel_all[..., frame_half:].astype(jnp.bfloat16), "section", 1).astype(
        jnp.float32
    )
    mel_out = jnp.where(is_first, mel_all[..., :frame_half], mel_moved)
    feature_half = model_width // 2
    cross_bias_all = summed[7][5]
    decoded_sent, text_sent, cross_sent = (
        shifted(decoded_all[..., :feature_half].astype(jnp.bfloat16), "section", -1).astype(
            jnp.float32
        ),
        shifted(text_all[..., :feature_half].astype(jnp.bfloat16), "section", -1).astype(
            jnp.float32
        ),
        shifted(cross_bias_all[:feature_half].astype(jnp.bfloat16), "section", -1).astype(
            jnp.float32
        ),
    )
    decoded_out = jnp.where(is_first, decoded_sent, decoded_all[..., feature_half:])
    text_out = jnp.where(is_first, text_sent, text_all[..., feature_half:])
    cross_bias_out = jnp.where(is_first, cross_sent, cross_bias_all[feature_half:])
    return (
        decoded_out,
        text_out,
        mel_out,
        conv_first_grad,
        conv_bias_grad,
        conv_second_grad,
        summed[0][None],
        summed[1][None],
        summed[2][None],
        summed[3][None],
        summed[4][None],
        summed[5][None],
        summed[6][None],
        summed[7][None],
        summed[8][None],
        summed[9][None],
        cross_bias_out,
    )


def solution(mesh):
    return jax.shard_map(
        shards,
        mesh=mesh,
        in_specs=(
            P("dp", None, None),
            P("dp"),
            P("dp"),
            P("dp"),
            P("dp"),
            P("dp"),
            P("dp", None, None),
            P("dp", None, None),
            P(),
            P(None, None, "section"),
            P("section"),
            P(None, None, "section"),
            P("section", None, None),
            P("section", None, None),
            P("section", None, None),
            P("section", None, None),
            P("section", None, None),
            P("section", None, None),
            P("section", None),
            P("section", None, None),
            P("section", None, None),
            P("section", None, None),
        ),
        out_specs=(
            P("dp", None, "section"),
            P("dp", None, "section"),
            P("dp", None, "section"),
            P(None, None, "section"),
            P("section"),
            P(None, None, "section"),
            P("section", None, None),
            P("section", None, None),
            P("section", None, None),
            P("section", None, None),
            P("section", None, None),
            P("section", None, None),
            P("section", None),
            P("section", None, None),
            P("section", None, None),
            P("section", None, None),
            P("section"),
        ),
        check_vma=False,
    )
```

profile of v0, /device:TPU:0, one launch (start us, length us, event | category | flops | bytes accessed | tf_op | source)
XLA Modules:
  0.0 1673.5 jit_solution(6797801881901624824)
XLA Ops:
  18.1 10.4 all_gather.9
  28.5 13.3 all-gather.3.cloned.1.call-done
  41.8 1242.0 %while.71 = (s32[]{:T(128)}, f32[3,512]{1,0:T(4,128)}, f32[3,512]{1,0:T(4,128)}, f32[512,1536]{0,1:T(8,128)}, f32[512,512]{0,1:T(8,128)}, /*index=5*/f32[512,204...) while((s32[]{:T(128)}, f32[3,512]{1,0:T(4,128)}, ...), condition=%wide.region_71.72_spmd.clone, body=%wide.region_0.71_spmd.clone.sunk | while | flops 46968700928 | bytes 1793299840 | solution.py:628
  52.6 97.9 %conditional.9 = (bf16[1024,512]{1,0:T(8,128)(2,1)}, bf16[1024,512]{1,0:T(8,128)(2,1)}, f32[2048,512]{1,0:T(8,128)}, bf16[2048,512]{1,0:T(8,128)(2,1)}, f32[1024...) conditional(s32[]{:T(128)} %convert_element_type.558, ...), branch_computations={%region_1.1_spmd, %region_2.12_spmd} | conditional | flops 10787495936 | bytes 279144896 | solution.py:588
  63.7 5.6 fusion.209
  98.6 22.9 %while.69 = (s32[]{:T(128)}, bf16[2,512,512]{2,1,0:T(8,128)(2,1)}, f32[2,8,512]{2,1,0:T(8,128)S(1)}, bf16[2,512,8,64]{1,3,2,0:T(8,128)(2,1)S(1)}, bf16[1024,8,64...) while((s32[]{:T(128)}, bf16[2,512,512]{2,1,0:T(8,128)(2,1)}, f32[2,8,512]{2,1,0:T(8,128)S(1)}, ...), condition=%wide.region_8.7_spmd, body=%wide.region_5.6_spmd.sunk | while | flops 1111748608 | bytes 59900528 | solution.py:192
  128.2 7.8 multiply_convert_fusion
  158.9 19.2 %collective-permute-done = bf16[1024,512]{0,1:T(8,128)(2,1)} collective-permute-done((bf16[1024,512]{0,1:T(8,128)(2,1)}, bf16[1024,512]{0,1:T(8,128)(2,1)}, u32[]{:S(2)}, u32[]{:S(2)}) %collective-permute-start) | collective-permute-done | bytes 1048608 | tf_op jit(solution)/shard_map/while/body/eval_jaxpr/ppermute | solution.py:17
  178.1 21.9 %collective-permute-done.1 = bf16[1024,512]{0,1:T(8,128)(2,1)S(1)} collective-permute-done((bf16[1024,512]{0,1:T(8,128)(2,1)}, bf16[1024,512]{0,1:T(8,128)(2,1)S(1)}, u32[]{:S(2)}, u32[]{:S(2)}) %collective-permute-start.1) | collective-permute-done | bytes 1048608 | tf_op jit(solution)/shard_map/while/body/eval_jaxpr/ppermute | solution.py:17
  200.0 16.7 %conditional.10 = (bf16[1024,512]{0,1:T(8,128)(2,1)S(1)}, bf16[1024,512]{0,1:T(8,128)(2,1)S(1)}, f32[3,512]{1,0:T(4,128)S(1)}, f32[3,512]{1,0:T(4,128)S(1)}, f32...) conditional(s32[]{:T(128)} %convert_element_type.558, ...), branch_computations={%region_13.44_spmd, %region_45.45_spmd} | conditional | flops 14080178176 | bytes 603845888 | solution.py:597
  226.4 133.8 %collective-permute-done.2 = bf16[1024,512]{1,0:T(8,128)(2,1)} collective-permute-done((bf16[1024,512]{1,0:T(8,128)(2,1)}, bf16[1024,512]{1,0:T(8,128)(2,1)}, u32[]{:S(2)}, u32[]{:S(2)}) %collective-permute-start.2) | collective-permute-done | bytes 1048608 | tf_op jit(solution)/shard_map/while/body/eval_jaxpr/ppermute | solution.py:17
  360.2 21.2 %collective-permute-done.3 = bf16[1024,512]{1,0:T(8,128)(2,1)S(1)} collective-permute-done((bf16[1024,512]{1,0:T(8,128)(2,1)}, bf16[1024,512]{1,0:T(8,128)(2,1)S(1)}, u32[]{:S(2)}, u32[]{:S(2)}) %collective-permute-start.3) | collective-permute-done | bytes 1048608 | tf_op jit(solution)/shard_map/while/body/eval_jaxpr/ppermute | solution.py:17
  381.4 241.2 %conditional.11 = (f32[3,512]{1,0:T(4,128)}, f32[3,512]{1,0:T(4,128)}, f32[512,1536]{0,1:T(8,128)}, f32[512,512]{0,1:T(8,128)}, f32[512,2048]{0,1:T(8,128)}, /*i...) conditional(s32[]{:T(128)} %convert_element_type.558, ...), branch_computations={%region_46.46_spmd, %region_47.70_spmd} | conditional | flops 22087675904 | bytes 674232704 | solution.py:616
  392.5 9.9 fusion.221
  405.2 6.9 multiply_reduce_fusion.21
  430.3 92.8 %while.70 = (s32[]{:T(128)}, f32[1024,8,64]{0,2,1:T(8,128)}, f32[1024,8,64]{0,2,1:T(8,128)}, f32[2,512,512]{1,2,0:T(8,128)}, bf16[2,512,8,64]{1,3,2,0:T(8,128)(2...) while((s32[]{:T(128)}, f32[1024,8,64]{0,2,1:T(8,128)}, ...), condition=%wide.region_54.53_spmd.clone, body=%wide.region_52.52_spmd.clone.sunk | while | flops 2737565696 | bytes 276940480 | solution.py:239
  434.0 10.8 multiply_reduce_fusion.28
  444.9 10.4 multiply_convert_fusion.8
  455.3 6.0 convolution_multiply_fusion.5
  462.4 6.6 bitcast_add_fusion.4
  479.4 10.8 multiply_reduce_fusion.28
  490.3 10.4 multiply_convert_fusion.8
  500.7 6.0 convolution_multiply_fusion.5
  507.8 7.2 bitcast_add_fusion.4
  517.5 5.7 bitcast_add_fusion.5
  555.6 6.1 reshape.467
  576.8 5.8 fusion.219
  603.8 5.9 convolution_bitcast_fusion.2
  609.7 6.6 convolution_bitcast_fusion.1
  632.5 6.3 fusion.348
  638.9 7.7 fusion.347
  672.7 97.9 %conditional.9 = (bf16[1024,512]{1,0:T(8,128)(2,1)}, bf16[1024,512]{1,0:T(8,128)(2,1)}, f32[2048,512]{1,0:T(8,128)}, bf16[2048,512]{1,0:T(8,128)(2,1)}, f32[1024...) conditional(s32[]{:T(128)} %convert_element_type.558, ...), branch_computations={%region_1.1_spmd, %region_2.12_spmd} | conditional | flops 10787495936 | bytes 279144896 | solution.py:588
  683.7 5.6 fusion.209
  718.7 22.9 %while.69 = (s32[]{:T(128)}, bf16[2,512,512]{2,1,0:T(8,128)(2,1)}, f32[2,8,512]{2,1,0:T(8,128)S(1)}, bf16[2,512,8,64]{1,3,2,0:T(8,128)(2,1)S(1)}, bf16[1024,8,64...) while((s32[]{:T(128)}, bf16[2,512,512]{2,1,0:T(8,128)(2,1)}, f32[2,8,512]{2,1,0:T(8,128)S(1)}, ...), condition=%wide.region_8.7_spmd, body=%wide.region_5.6_spmd.sunk | while | flops 1111748608 | bytes 59900528 | solution.py:192
  748.3 7.8 multiply_convert_fusion
  778.9 19.3 %collective-permute-done = bf16[1024,512]{0,1:T(8,128)(2,1)} collective-permute-done((bf16[1024,512]{0,1:T(8,128)(2,1)}, bf16[1024,512]{0,1:T(8,128)(2,1)}, u32[]{:S(2)}, u32[]{:S(2)}) %collective-permute-start) | collective-permute-done | bytes 1048608 | tf_op jit(solution)/shard_map/while/body/eval_jaxpr/ppermute | solution.py:17
  798.3 20.6 %collective-permute-done.1 = bf16[1024,512]{0,1:T(8,128)(2,1)S(1)} collective-permute-done((bf16[1024,512]{0,1:T(8,128)(2,1)}, bf16[1024,512]{0,1:T(8,128)(2,1)S(1)}, u32[]{:S(2)}, u32[]{:S(2)}) %collective-permute-start.1) | collective-permute-done | bytes 1048608 | tf_op jit(solution)/shard_map/while/body/eval_jaxpr/ppermute | solution.py:17
  818.9 16.7 %conditional.10 = (bf16[1024,512]{0,1:T(8,128)(2,1)S(1)}, bf16[1024,512]{0,1:T(8,128)(2,1)S(1)}, f32[3,512]{1,0:T(4,128)S(1)}, f32[3,512]{1,0:T(4,128)S(1)}, f32...) conditional(s32[]{:T(128)} %convert_element_type.558, ...), branch_computations={%region_13.44_spmd, %region_45.45_spmd} | conditional | flops 14080178176 | bytes 603845888 | solution.py:597
  845.4 133.7 %collective-permute-done.2 = bf16[1024,512]{1,0:T(8,128)(2,1)} collective-permute-done((bf16[1024,512]{1,0:T(8,128)(2,1)}, bf16[1024,512]{1,0:T(8,128)(2,1)}, u32[]{:S(2)}, u32[]{:S(2)}) %collective-permute-start.2) | collective-permute-done | bytes 1048608 | tf_op jit(solution)/shard_map/while/body/eval_jaxpr/ppermute | solution.py:17
  979.1 19.9 %collective-permute-done.3 = bf16[1024,512]{1,0:T(8,128)(2,1)S(1)} collective-permute-done((bf16[1024,512]{1,0:T(8,128)(2,1)}, bf16[1024,512]{1,0:T(8,128)(2,1)S(1)}, u32[]{:S(2)}, u32[]{:S(2)}) %collective-permute-start.3) | collective-permute-done | bytes 1048608 | tf_op jit(solution)/shard_map/while/body/eval_jaxpr/ppermute | solution.py:17
  998.9 241.2 %conditional.11 = (f32[3,512]{1,0:T(4,128)}, f32[3,512]{1,0:T(4,128)}, f32[512,1536]{0,1:T(8,128)}, f32[512,512]{0,1:T(8,128)}, f32[512,2048]{0,1:T(8,128)}, /*i...) conditional(s32[]{:T(128)} %convert_element_type.558, ...), branch_computations={%region_46.46_spmd, %region_47.70_spmd} | conditional | flops 22087675904 | bytes 674232704 | solution.py:616
  1010.0 9.8 fusion.221
  1022.8 6.9 multiply_reduce_fusion.21
  1047.8 92.8 %while.70 = (s32[]{:T(128)}, f32[1024,8,64]{0,2,1:T(8,128)}, f32[1024,8,64]{0,2,1:T(8,128)}, f32[2,512,512]{1,2,0:T(8,128)}, bf16[2,512,8,64]{1,3,2,0:T(8,128)(2...) while((s32[]{:T(128)}, f32[1024,8,64]{0,2,1:T(8,128)}, ...), condition=%wide.region_54.53_spmd.clone, body=%wide.region_52.52_spmd.clone.sunk | while | flops 2737565696 | bytes 276940480 | solution.py:239
  1051.5 10.8 multiply_reduce_fusion.28
  1062.4 10.4 multiply_convert_fusion.8
  1072.9 6.0 convolution_multiply_fusion.5
  1080.0 6.6 bitcast_add_fusion.4
  1096.9 10.8 multiply_reduce_fusion.28
  1107.9 10.4 multiply_convert_fusion.8
  1118.3 6.0 convolution_multiply_fusion.5
  1125.4 7.2 bitcast_add_fusion.4
  1135.0 5.7 bitcast_add_fusion.5
  1173.1 6.1 reshape.467
  1194.4 5.8 fusion.219
  1221.4 5.9 convolution_bitcast_fusion.2
  1227.2 6.6 convolution_bitcast_fusion.1
  1242.1 5.5 select_add_fusion.18
  1251.0 6.3 fusion.348
  1257.4 7.7 fusion.347
  1289.3 5.5 copy.253
  1300.4 62.8 %all-reduce.7 = (f32[512]{0:T(512)S(1)}, f32[1,3,512]{2,0,1:T(1,128)}, f32[1,3,512]{2,0,1:T(1,128)}, f32[1,2048]{1,0:T(1,128)}, f32[6,512]{1,0:T(8,128)S(1)}) all-reduce(f32[512]{0:T(512)S(1)} %copy-done.135, f32[1,3,512]{2,0,1:T(1,128)S(1)} %broadcast_in_dim.287, ...), channel_id=1, replica_groups=mesh['section'=2,'dp'=16] {'dp'}, use_global_device_ids=true, to_apply=%region_73.74 | all-reduce | flops 8704 | bytes 69632 | tf_op jit(solution)/shard_map/psum | solution.py:642
  1378.5 249.2 %all-reduce.11.cloned.1.call-done = (f32[3,80,512]{2,1,0:T(8,128)}, f32[3,512,512]{2,1,0:T(8,128)}, f32[1,512,1536]{2,1,0:T(8,128)}, f32[1,512,512]{2,1,0:T(8,12...) async-done(((f32[3,80,512]{2,1,0:T(8,128)}, f32[3,512,512]{2,1,0:T(8,128)}, f32[1,512,1536]{2,1,0:T(8,128)}, ...) | async-done | bytes 18317328 | tf_op jit(solution)/shard_map/psum | solution.py:642
  1638.8 13.5 collective-permute-done.7
  (824 shorter events, 602.5 us)
Async XLA Ops:
  7.2 34.6 %all-gather.3.cloned.1.call-start = ((), (), s32[]{:S(2)}) async-start(), calls=%async_computation | async-start | bytes 2359296 | tf_op jit(solution)/shard_map/all_gather | solution.py:560
  7.9 1619.7 %all-reduce.11.cloned.1.call-start = ((), (), s32[]{:S(2)}) async-start(), calls=%async_computation.1 | async-start | bytes 36634624 | tf_op jit(solution)/shard_map/psum | solution.py:642
  61.1 8.2 copy-start.12
  98.6 23.0 %copy-start.126 = (f32[1,512]{1,0:T(1,128)S(1)}, f32[1,512]{1,0:T(1,128)}, u32[]{:S(2)}) copy-start(f32[1,512]{1,0:T(1,128)} %get-tuple-element.1613) | copy-start | bytes 6148 | tf_op jit(solution)/shard_map/while/body/eval_jaxpr/cond
  128.2 7.8 copy-start.141
  150.5 49.5 %copy-start.97 = (f32[1024,1]{0,1:T(1,128)}, f32[1024,1]{0,1:T(1,128)S(1)}, u32[]{:S(2)}) copy-start(f32[1024,1]{0,1:T(1,128)S(1)} %get-tuple-element.2103) | copy-start | bytes 12292 | tf_op jit(solution)/shard_map/while
  150.5 49.5 %copy-start.22 = (bf16[512,512]{1,0:T(8,128)(2,1)S(1)}, bf16[512,512]{1,0:T(8,128)(2,1)}, u32[]{:S(2)}) copy-start(bf16[512,512]{1,0:T(8,128)(2,1)} %get-tuple-element.2425) | copy-start | bytes 1572868 | tf_op jit(solution)/shard_map/while
  150.5 49.4 %copy-start.35 = (bf16[512,512]{1,0:T(8,128)(2,1)S(1)}, bf16[512,512]{1,0:T(8,128)(2,1)}, u32[]{:S(2)}) copy-start(bf16[512,512]{1,0:T(8,128)(2,1)} %get-tuple-element.2430) | copy-start | bytes 1572868 | tf_op jit(solution)/shard_map/while
  150.5 49.4 %copy-start.50 = (bf16[2,448,512]{2,1,0:T(8,128)(2,1)S(1)}, bf16[2,448,512]{2,1,0:T(8,128)(2,1)}, u32[]{:S(2)}) copy-start(bf16[2,448,512]{2,1,0:T(8,128)(2,1)} %get-tuple-element.2431) | copy-start | bytes 2752516 | tf_op jit(solution)/shard_map/while
  150.5 49.4 %copy-start.107 = (bf16[2048]{0:T(1024)(128)(2,1)S(1)}, bf16[2048]{0:T(1024)(128)(2,1)}, u32[]{:S(2)}) copy-start(bf16[2048]{0:T(1024)(128)(2,1)} %get-tuple-element.2427) | copy-start | bytes 12292 | tf_op jit(solution)/shard_map/while
  150.5 49.4 %copy-start.149 = (s32[2]{0:T(128)S(1)}, s32[2]{0:T(128)}, u32[]{:S(2)}) copy-start(s32[2]{0:T(128)} %get-tuple-element.2432) | copy-start | bytes 28 | tf_op jit(solution)/shard_map/while
  153.0 25.1 %collective-permute-start = (bf16[1024,512]{0,1:T(8,128)(2,1)}, bf16[1024,512]{0,1:T(8,128)(2,1)}, u32[]{:S(2)}, u32[]{:S(2)}) collective-permute-start(bf16[1024,512]{0,1:T(8,128)(2,1)} %copy.301), channel_id=1, source_target_pairs={{0,16},{1,17},{2,18},{3,19},{4,20},{5,21},{6,22},{7,23},{8,24},{9,... | collective-permute-start | bytes 3145736 | tf_op jit(solution)/shard_map/while/body/eval_jaxpr/ppermute | solution.py:17
  157.5 42.4 %collective-permute-start.1 = (bf16[1024,512]{0,1:T(8,128)(2,1)}, bf16[1024,512]{0,1:T(8,128)(2,1)S(1)}, u32[]{:S(2)}, u32[]{:S(2)}) collective-permute-start(bf16[1024,512]{0,1:T(8,128)(2,1)} %copy.302), channel_id=1, source_target_pairs={{0,16},{1,17},{2,18},{3,19},{4,20},{5,21},{6,22},{7,23},{8,24},{9,... | collective-permute-start | bytes 3145736 | tf_op jit(solution)/shard_map/while/body/eval_jaxpr/ppermute | solution.py:17
  216.8 9.7 copy-start.130
  218.7 162.7 %copy-start.23 = (bf16[512,512]{1,0:T(8,128)(2,1)S(1)}, bf16[512,512]{1,0:T(8,128)(2,1)}, u32[]{:S(2)}) copy-start(bf16[512,512]{1,0:T(8,128)(2,1)} %get-tuple-element.2425) | copy-start | bytes 1572868 | tf_op jit(solution)/shard_map/while
  218.7 162.7 %copy-start.36 = (bf16[512,512]{1,0:T(8,128)(2,1)S(1)}, bf16[512,512]{1,0:T(8,128)(2,1)}, u32[]{:S(2)}) copy-start(bf16[512,512]{1,0:T(8,128)(2,1)} %get-tuple-element.2430) | copy-start | bytes 1572868 | tf_op jit(solution)/shard_map/while
  218.7 141.6 %collective-permute-start.2 = (bf16[1024,512]{1,0:T(8,128)(2,1)}, bf16[1024,512]{1,0:T(8,128)(2,1)}, u32[]{:S(2)}, u32[]{:S(2)}) collective-permute-start(bf16[1024,512]{1,0:T(8,128)(2,1)} %copy.303), channel_id=1, source_target_pairs={{16,0},{17,1},{18,2},{19,3},{20,4},{21,5},{22,6},{23,7},{24,8},{25... | collective-permute-start | bytes 3145736 | tf_op jit(solution)/shard_map/while/body/eval_jaxpr/ppermute | solution.py:17
  221.4 160.0 %collective-permute-start.3 = (bf16[1024,512]{1,0:T(8,128)(2,1)}, bf16[1024,512]{1,0:T(8,128)(2,1)S(1)}, u32[]{:S(2)}, u32[]{:S(2)}) collective-permute-start(bf16[1024,512]{1,0:T(8,128)(2,1)} %copy.304), channel_id=1, source_target_pairs={{16,0},{17,1},{18,2},{19,3},{20,4},{21,5},{22,6},{23,7},{24,8},{25... | collective-permute-start | bytes 3145736 | tf_op jit(solution)/shard_map/while/body/eval_jaxpr/ppermute | solution.py:17
  392.5 19.6 %copy-start.9 = (f32[1024,512]{1,0:T(8,128)}, f32[1024,512]{1,0:T(8,128)S(1)}, u32[]{:S(2)}) copy-start(f32[1024,512]{1,0:T(8,128)S(1)} %get-tuple-element.1600) | copy-start | bytes 6291460 | tf_op jit(solution)/shard_map/while/body/eval_jaxpr/cond
  433.9 11.0 copy-start
  462.4 9.1 copy-start.1
  479.4 11.0 copy-start
  507.8 9.7 copy-start.1
  530.4 9.5 copy-start.69
  624.6 7.9 copy-start.29
  630.3 8.5 copy-start.76
  646.6 9.1 copy-start.28
  681.2 8.2 copy-start.12
  718.7 23.0 %copy-start.126 = (f32[1,512]{1,0:T(1,128)S(1)}, f32[1,512]{1,0:T(1,128)}, u32[]{:S(2)}) copy-start(f32[1,512]{1,0:T(1,128)} %get-tuple-element.1613) | copy-start | bytes 6148 | tf_op jit(solution)/shard_map/while/body/eval_jaxpr/cond
  770.6 48.4 %copy-start.97 = (f32[1024,1]{0,1:T(1,128)}, f32[1024,1]{0,1:T(1,128)S(1)}, u32[]{:S(2)}) copy-start(f32[1024,1]{0,1:T(1,128)S(1)} %get-tuple-element.2103) | copy-start | bytes 12292 | tf_op jit(solution)/shard_map/while
  770.6 48.3 %copy-start.22 = (bf16[512,512]{1,0:T(8,128)(2,1)S(1)}, bf16[512,512]{1,0:T(8,128)(2,1)}, u32[]{:S(2)}) copy-start(bf16[512,512]{1,0:T(8,128)(2,1)} %get-tuple-element.2425) | copy-start | bytes 1572868 | tf_op jit(solution)/shard_map/while
  770.6 48.3 %copy-start.35 = (bf16[512,512]{1,0:T(8,128)(2,1)S(1)}, bf16[512,512]{1,0:T(8,128)(2,1)}, u32[]{:S(2)}) copy-start(bf16[512,512]{1,0:T(8,128)(2,1)} %get-tuple-element.2430) | copy-start | bytes 1572868 | tf_op jit(solution)/shard_map/while
  770.6 48.3 %copy-start.50 = (bf16[2,448,512]{2,1,0:T(8,128)(2,1)S(1)}, bf16[2,448,512]{2,1,0:T(8,128)(2,1)}, u32[]{:S(2)}) copy-start(bf16[2,448,512]{2,1,0:T(8,128)(2,1)} %get-tuple-element.2431) | copy-start | bytes 2752516 | tf_op jit(solution)/shard_map/while
  770.6 48.3 %copy-start.107 = (bf16[2048]{0:T(1024)(128)(2,1)S(1)}, bf16[2048]{0:T(1024)(128)(2,1)}, u32[]{:S(2)}) copy-start(bf16[2048]{0:T(1024)(128)(2,1)} %get-tuple-element.2427) | copy-start | bytes 12292 | tf_op jit(solution)/shard_map/while
  770.6 48.3 %copy-start.149 = (s32[2]{0:T(128)S(1)}, s32[2]{0:T(128)}, u32[]{:S(2)}) copy-start(s32[2]{0:T(128)} %get-tuple-element.2432) | copy-start | bytes 28 | tf_op jit(solution)/shard_map/while
  773.1 25.2 %collective-permute-start = (bf16[1024,512]{0,1:T(8,128)(2,1)}, bf16[1024,512]{0,1:T(8,128)(2,1)}, u32[]{:S(2)}, u32[]{:S(2)}) collective-permute-start(bf16[1024,512]{0,1:T(8,128)(2,1)} %copy.301), channel_id=1, source_target_pairs={{0,16},{1,17},{2,18},{3,19},{4,20},{5,21},{6,22},{7,23},{8,24},{9,... | collective-permute-start | bytes 3145736 | tf_op jit(solution)/shard_map/while/body/eval_jaxpr/ppermute | solution.py:17
  777.6 41.3 %collective-permute-start.1 = (bf16[1024,512]{0,1:T(8,128)(2,1)}, bf16[1024,512]{0,1:T(8,128)(2,1)S(1)}, u32[]{:S(2)}, u32[]{:S(2)}) collective-permute-start(bf16[1024,512]{0,1:T(8,128)(2,1)} %copy.302), channel_id=1, source_target_pairs={{0,16},{1,17},{2,18},{3,19},{4,20},{5,21},{6,22},{7,23},{8,24},{9,... | collective-permute-start | bytes 3145736 | tf_op jit(solution)/shard_map/while/body/eval_jaxpr/ppermute | solution.py:17
  835.7 9.7 copy-start.130
  837.6 161.3 %copy-start.23 = (bf16[512,512]{1,0:T(8,128)(2,1)S(1)}, bf16[512,512]{1,0:T(8,128)(2,1)}, u32[]{:S(2)}) copy-start(bf16[512,512]{1,0:T(8,128)(2,1)} %get-tuple-element.2425) | copy-start | bytes 1572868 | tf_op jit(solution)/shard_map/while
  837.6 161.3 %copy-start.36 = (bf16[512,512]{1,0:T(8,128)(2,1)S(1)}, bf16[512,512]{1,0:T(8,128)(2,1)}, u32[]{:S(2)}) copy-start(bf16[512,512]{1,0:T(8,128)(2,1)} %get-tuple-element.2430) | copy-start | bytes 1572868 | tf_op jit(solution)/shard_map/while
  837.6 141.4 %collective-permute-start.2 = (bf16[1024,512]{1,0:T(8,128)(2,1)}, bf16[1024,512]{1,0:T(8,128)(2,1)}, u32[]{:S(2)}, u32[]{:S(2)}) collective-permute-start(bf16[1024,512]{1,0:T(8,128)(2,1)} %copy.303), channel_id=1, source_target_pairs={{16,0},{17,1},{18,2},{19,3},{20,4},{21,5},{22,6},{23,7},{24,8},{25... | collective-permute-start | bytes 3145736 | tf_op jit(solution)/shard_map/while/body/eval_jaxpr/ppermute | solution.py:17
  840.4 158.6 %collective-permute-start.3 = (bf16[1024,512]{1,0:T(8,128)(2,1)}, bf16[1024,512]{1,0:T(8,128)(2,1)S(1)}, u32[]{:S(2)}, u32[]{:S(2)}) collective-permute-start(bf16[1024,512]{1,0:T(8,128)(2,1)} %copy.304), channel_id=1, source_target_pairs={{16,0},{17,1},{18,2},{19,3},{20,4},{21,5},{22,6},{23,7},{24,8},{25... | collective-permute-start | bytes 3145736 | tf_op jit(solution)/shard_map/while/body/eval_jaxpr/ppermute | solution.py:17
  1010.0 19.6 %copy-start.9 = (f32[1024,512]{1,0:T(8,128)}, f32[1024,512]{1,0:T(8,128)S(1)}, u32[]{:S(2)}) copy-start(f32[1024,512]{1,0:T(8,128)S(1)} %get-tuple-element.1600) | copy-start | bytes 6291460 | tf_op jit(solution)/shard_map/while/body/eval_jaxpr/cond
  1051.5 11.0 copy-start
  1079.9 9.1 copy-start.1
  1096.9 11.0 copy-start
  1125.4 9.7 copy-start.1
  1147.9 9.5 copy-start.69
  1242.1 8.2 copy-start.111
  1242.1 8.2 copy-start.131
  1242.1 8.9 copy-start.29
  1248.8 8.5 copy-start.76
  1265.1 9.1 copy-start.28
  1299.7 66.7 %copy-start.103 = (f32[2,80,2048]{2,1,0:T(8,128)S(1)}, f32[2,80,2048]{2,1,0:T(8,128)}, u32[]{:S(2)}) copy-start(f32[2,80,2048]{2,1,0:T(8,128)} %get-tuple-element.728) | copy-start | bytes 3932164
  1299.7 74.6 %copy-start.94 = (f32[2,448,512]{2,1,0:T(8,128)S(1)}, f32[2,448,512]{2,1,0:T(8,128)}, u32[]{:S(2)}) copy-start(f32[2,448,512]{2,1,0:T(8,128)} %get-tuple-element.726) | copy-start | bytes 5505028
  1363.8 12.6 collective-permute-start.8
  1365.1 11.9 collective-permute-start.10
  1366.4 11.1 collective-permute-start.6
  1373.0 259.7 %collective-permute-start.5 = (bf16[2,448,256]{2,1,0:T(8,128)(2,1)}, bf16[2,448,256]{2,1,0:T(8,128)(2,1)}, u32[]{:S(2)}, u32[]{:S(2)}) collective-permute-start(bf16[2,448,256]{2,1,0:T(8,128)(2,1)} %slice.425), channel_id=1, source_target_pairs={{16,0},{17,1},{18,2},{19,3},{20,4},{21,5},{22,6},{23,7},{24,8},{25... | collective-permute-start | bytes 1376264 | tf_op jit(solution)/shard_map/ppermute | solution.py:17
  1375.1 261.6 %collective-permute-start.4 = (bf16[2,448,256]{2,1,0:T(8,128)(2,1)}, bf16[2,448,256]{2,1,0:T(8,128)(2,1)}, u32[]{:S(2)}, u32[]{:S(2)}) collective-permute-start(bf16[2,448,256]{2,1,0:T(8,128)(2,1)} %slice.426), channel_id=1, source_target_pairs={{16,0},{17,1},{18,2},{19,3},{20,4},{21,5},{22,6},{23,7},{24,8},{25... | collective-permute-start | bytes 1376264 | tf_op jit(solution)/shard_map/ppermute | solution.py:17
  1627.6 25.5 %copy-start.88 = (f32[3,512,512]{2,1,0:T(8,128)S(1)}, f32[3,512,512]{2,1,0:T(8,128)}, u32[]{:S(2)}) copy-start(f32[3,512,512]{2,1,0:T(8,128)} %get-tuple-element.1576) | copy-start | bytes 9437188
  1629.3 23.8 %collective-permute-start.9 = (bf16[3,512,256]{2,1,0:T(8,128)(2,1)S(1)}, bf16[3,512,256]{2,1,0:T(8,128)(2,1)S(1)}, u32[]{:S(2)}, u32[]{:S(2)}) collective-permute-start(bf16[3,512,256]{2,1,0:T(8,128)(2,1)S(1)} %slice.424), channel_id=1, source_target_pairs={{0,16},{1,17},{2,18},{3,19},{4,20},{5,21},{6,22},{7,23},{8,24},{9,... | collective-permute-start | bytes 2359304 | tf_op jit(solution)/shard_map/ppermute | solution.py:17
  1635.1 19.4 %copy-start.87 = (f32[1,512,1536]{2,1,0:T(8,128)S(1)}, f32[1,512,1536]{2,1,0:T(8,128)}, u32[]{:S(2)}) copy-start(f32[1,512,1536]{2,1,0:T(8,128)} %get-tuple-element.2444) | copy-start | bytes 9437188
  1635.1 17.3 %collective-permute-start.7 = (bf16[3,80,256]{2,1,0:T(8,128)(2,1)S(1)}, bf16[3,80,256]{2,1,0:T(8,128)(2,1)S(1)}, u32[]{:S(2)}, u32[]{:S(2)}) collective-permute-start(bf16[3,80,256]{2,1,0:T(8,128)(2,1)S(1)} %slice.428), channel_id=1, source_target_pairs={{0,16},{1,17},{2,18},{3,19},{4,20},{5,21},{6,22},{7,23},{8,24},{9,... | collective-permute-start | bytes 368648 | tf_op jit(solution)/shard_map/ppermute | solution.py:17
  (173 other events, 737.0 us)
Sparse Core Ops, SparseCore 0:
  9.6 32.2 all-gather.2
  1299.8 327.7 all-reduce.10
where the time goes:
time: 1680 us; the launch traced here: 1670 us
  waiting for transfers between devices  666 us (40%)
  matrix products  361 us (21%)
  local copies, waits for them, and re-layouts  272 us (16%)
  other arithmetic  231 us (14%)
  blocking collectives  78.3 us (5%)
  starting transfers between devices  27.4 us (2%)
  loops' own time  22.1 us (1%)
    ppermute x15, waiting for transfers between devices, shifted(): return lax.ppermute(shard, axis, pairs)  403 us
    psum x1, waiting for transfers between devices, shards(): lax.psum((layer_totals[0], layer_totals[1], layer_totals[2], layer_totals...  249 us
    psum x1, blocking collectives, shards(): lax.psum((layer_totals[0], layer_totals[1], layer_totals[2], layer_totals...  62.8 us
    dot_general x18, matrix products, input_grad(): lax.dot_general(grad_low, weight, (((1,), (1,)), ((), ())), preferred_ele...  59.4 us
    add x16, other arithmetic, clip_step(): total_now + first_now + second_now  58.8 us
    dot_general x18, matrix products, matmul(): return jnp.dot(left, right, preferred_element_type=jnp.float32)  58.7 us
    dot_general x18, matrix products, weight_grad(): lax.dot_general(inputs, grad_low, (((0,), (0,)), ((), ())), preferred_ele...  58 us
    dot_general x4, matrix products, one_block(): jnp.einsum('qhd,khd->hqk', grad_block, value_heads, preferred_element_typ...  43 us
  transfers between devices with their start and end apart: 17, of which 11 were waited for; matrix products, arithmetic and copies ran while one was open for 2% of the time, Pallas kernels for 0%

commit v1 on v0

--- a/solution.py
+++ b/solution.py
@@ -545,170 +545,110 @@
         cross_first[0],
         cross_second[0],
     )
-    frame_count = positions.shape[0]
-    model_width = positions.shape[1]
-    hidden_width = mlp_up.shape[2]
-    band_count = mel_input.shape[1]
+    section_at = lax.axis_index("section")
+
+    def both(weight):
+        return lax.all_gather(weight, "section", axis=0, tiled=False)
+
+    gathered = tuple(both(weight) for weight in weights)
+    audio_weights = tuple(weight[0] for weight in gathered)
+    text_weights = tuple(weight[1] for weight in gathered)
+    first_all = lax.all_gather(conv_first, "section", axis=2, tiled=True)
+    bias_all = lax.all_gather(conv_first_bias, "section", axis=0, tiled=True)
+    second_all = lax.all_gather(conv_second, "section", axis=2, tiled=True)
+
+    def own(array):
+        return lax.dynamic_index_in_dim(array, section_at, 0, keepdims=False)
+
+    mel_clip, text_clip, cot_clip = own(mel_input), own(text_embed), own(cotangent)
     mel_frames = mel_input.shape[2]
-    text_rows = text_embed.shape[1]
-    blank_memory = jnp.zeros((frame_count, model_width), jnp.bfloat16)
-    blank_text = jnp.zeros((text_rows, model_width), jnp.float32)
-    blank_grads = tuple((jnp.zeros(weight.shape, jnp.float32) for weight in weights))
-    first_all, bias_all, second_all = (
-        lax.all_gather(conv_first, "section", axis=2, tiled=True),
-        lax.all_gather(conv_first_bias, "section", axis=0, tiled=True),
-        lax.all_gather(conv_second, "section", axis=2, tiled=True),
-    )
-    stem_shapes = (first_all.shape, bias_all.shape, second_all.shape)
-    blank_mel = jnp.zeros((band_count, mel_frames), jnp.float32)
-    blank_stem = tuple((jnp.zeros(shape_now, jnp.float32) for shape_now in stem_shapes))
-
-    def clip_step(running, item):
-        layer_totals, stem_totals = running
-        mel_clip, time_begin, time_span, band_begin, band_span, text_length, text_clip, cot_clip = (
-            item
+    keep = spec_keep(
+        own(time_start), own(time_width), own(freq_start), own(freq_width), mel_input.shape[1], mel_frames
+    )
+    masked = jnp.where(keep, mel_clip, jnp.zeros_like(mel_clip))
+    pre_act, hidden = stem_first(masked, first_all, bias_all)
+    conv_out = stem_second(hidden, second_all)
+    memory_keys, memory_values, kept = encode(conv_out, positions, audio_weights)
+    decoded, text_grad, keys_back, values_back, text_grads = decode(
+        text_clip, cot_clip, own(text_len), memory_keys, memory_values, text_weights
+    )
+    audio_grads, grad_second = encode_back(keys_back, values_back, kept, audio_weights)
+    second_low = grad_second.astype(jnp.bfloat16)
+    grad_conv_second, grad_hidden = stem_second_back(hidden, second_all, second_low)
+    grad_conv_first, grad_conv_bias, grad_masked = stem_first_back(
+        masked, first_all, pre_act, grad_hidden
+    )
+    mel_grad = jnp.where(keep, grad_masked, 0.0)
+
+    half = first_all.shape[2] // 2
+
+    def halves(array):
+        return jnp.stack([array[..., :half], array[..., half:]])
+
+    big = [
+        jnp.stack([audio_grads[n], text_grads[n]]) for n in (2, 3, 4, 5, 8, 9)
+    ] + [halves(grad_conv_first), halves(grad_conv_second)]
+    small = [jnp.stack([audio_grads[n], text_grads[n]]) for n in (0, 1, 6, 7)] + [
+        halves(grad_conv_bias)
+    ]
+    flat = jnp.concatenate(
+        [array.reshape(2, -1, 512).astype(jnp.bfloat16) for array in big], axis=1
+    )
+    pad = -flat.shape[1] % (16 * lax.axis_size("dp"))
+    flat = jnp.pad(flat, ((0, 0), (0, pad), (0, 0)))
+    flat_shard = lax.psum_scatter(
+        flat, "section", scatter_dimension=0, tiled=False
+    )
+    flat_all = lax.psum(flat_shard, "dp").astype(jnp.float32)
+    small_flat = jnp.concatenate([array.reshape(2, -1) for array in small], axis=1)
+    small_all = lax.psum(
+        lax.psum_scatter(small_flat, "section", scatter_dimension=0, tiled=False), "dp"
+    )
+    outs, at = [], 0
+    for array in big:
+        rows = array.size // 1024
+        outs.append(flat_all[at : at + rows].reshape(array.shape[1:]))
+        at += rows
+    smalls, at = [], 0
+    for array in small:
+        count = array.size // 2
+        smalls.append(small_all[at : at + count].reshape(array.shape[1:]))
+        at += count
+
+    def swap(array, axis):
+        size = array.shape[axis] // 2
+        first = lax.slice_in_dim(array, 0, size, axis=axis)
+        second = lax.slice_in_dim(array, size, 2 * size, axis=axis)
+        is_first = section_at == 0
+        keep_part = jnp.where(is_first, first, second)
+        send_part = jnp.where(is_first, second, first).astype(jnp.bfloat16)
+        got = lax.ppermute(send_part, "section", [(0, 1), (1, 0)]).astype(jnp.float32)
+        return jnp.where(
+            is_first, jnp.stack([keep_part, got]), jnp.stack([got, keep_part])
         )
-        keep = spec_keep(time_begin, time_span, band_begin, band_span, band_count, mel_frames)
-        masked = jnp.where(keep, mel_clip, jnp.zeros_like(mel_clip))
-
-        def forward_first():
-            pre_act, hidden = stem_first(masked, first_all, bias_all)
-            conv_out = stem_second(hidden, second_all)
-            memory_keys, memory_values, kept = encode(conv_out, positions, weights)
-            return (memory_keys, memory_values, (pre_act, hidden, kept))
-
-        def forward_blank():
-            blank_keys, blank_values, blank_kept = blank_encode(
-                frame_count, model_width, hidden_width
-            )
-            stem_pre = jnp.zeros((mel_frames, model_width), jnp.float32)
-            stem_hidden = jnp.zeros((mel_frames, model_width), jnp.bfloat16)
-            return (blank_keys, blank_values, (stem_pre, stem_hidden, blank_kept))
-
-        memory_keys, memory_values, saved = lax.cond(is_first, forward_first, forward_blank)
-        keys_in, values_in = shifted((memory_keys, memory_values), "section", 1)
-
-        def second_section():
-            return decode(text_clip, cot_clip, text_length, keys_in, values_in, weights)
-
-        def second_blank():
-            return (blank_text, blank_text, blank_memory, blank_memory, blank_grads)
-
-        decoded, text_grad, grad_keys, grad_values, second_grads = lax.cond(
-            is_first, second_blank, second_section
-        )
-        keys_back, values_back = shifted((grad_keys, grad_values), "section", -1)
-
-        def first_back():
-            pre_act, hidden, kept = saved
-            first_grads, grad_second = encode_back(keys_back, values_back, kept, weights)
-            second_low = grad_second.astype(jnp.bfloat16)
-            grad_conv_second, grad_hidden = stem_second_back(hidden, second_all, second_low)
-            grad_conv_first, grad_conv_bias, grad_masked = stem_first_back(
-                masked, first_all, pre_act, grad_hidden
-            )
-            return (
-                first_grads,
-                (grad_conv_first, grad_conv_bias, grad_conv_second),
-                jnp.where(keep, grad_masked, 0.0),
-            )
-
-        first_grads, stem_grads, mel_grad = lax.cond(
-            is_first, first_back, lambda: (blank_grads, blank_stem, blank_mel)
-        )
-        layer_totals = jax.tree.map(
-            lambda total_now, first_now, second_now: total_now + first_now + second_now,
-            layer_totals,
-            first_grads,
-            second_grads,
-        )
-        stem_totals = jax.tree.map(jnp.add, stem_totals, stem_grads)
-        return ((layer_totals, stem_totals), (decoded, text_grad, mel_grad))
-
-    (layer_totals, stem_totals), (decoded_all, text_all, mel_all) = lax.scan(
-        clip_step,
-        (blank_grads, blank_stem),
-        (
-            mel_input,
-            time_start,
-            time_width,
-            freq_start,
-            freq_width,
-            text_len,
-            text_embed,
-            cotangent,
-        ),
-    )
-    summed = lax.psum(
-        (
-            layer_totals[0],
-            layer_totals[1],
-            layer_totals[2],
-            layer_totals[3],
-            layer_totals[4],
-            layer_totals[5],
-            layer_totals[6],
-            layer_totals[7],
-            layer_totals[8],
-            layer_totals[9],
-            stem_totals[0],
-            stem_totals[1],
-            stem_totals[2],
-        ),
-        "dp",
-    )
-    channel_half = model_width // 2
-    moved_first, moved_bias, moved_second = (
-        shifted(summed[10][..., channel_half:].astype(jnp.bfloat16), "section", 1).astype(
-            jnp.float32
-        ),
-        shifted(summed[11][channel_half:].astype(jnp.bfloat16), "section", 1).astype(jnp.float32),
-        shifted(summed[12][..., channel_half:].astype(jnp.bfloat16), "section", 1).astype(
-            jnp.float32
-        ),
-    )
-    conv_first_grad = jnp.where(is_first, summed[10][..., :channel_half], moved_first)
-    conv_bias_grad = jnp.where(is_first, summed[11][:channel_half], moved_bias)
-    conv_second_grad = jnp.where(is_first, summed[12][..., :channel_half], moved_second)
-    frame_half = mel_frames // 2
-    mel_moved = shifted(mel_all[..., frame_half:].astype(jnp.bfloat16), "section", 1).astype(
-        jnp.float32
-    )
-    mel_out = jnp.where(is_first, mel_all[..., :frame_half], mel_moved)
-    feature_half = model_width // 2
-    cross_bias_all = summed[7][5]
-    decoded_sent, text_sent, cross_sent = (
-        shifted(decoded_all[..., :feature_half].astype(jnp.bfloat16), "section", -1).astype(
-            jnp.float32
-        ),
-        shifted(text_all[..., :feature_half].astype(jnp.bfloat16), "section", -1).astype(
-            jnp.float32
-        ),
-        shifted(cross_bias_all[:feature_half].astype(jnp.bfloat16), "section", -1).astype(
-            jnp.float32
-        ),
-    )
-    decoded_out = jnp.where(is_first, decoded_sent, decoded_all[..., feature_half:])
-    text_out = jnp.where(is_first, text_sent, text_all[..., feature_half:])
-    cross_bias_out = jnp.where(is_first, cross_sent, cross_bias_all[feature_half:])
+
+    cross_all = lax.ppermute(smalls[3][5].astype(jnp.bfloat16), "section", [(1, 0)])
+    cross_row = jnp.where(section_at == 0, cross_all.astype(jnp.float32), smalls[3][5])
+    cross_half = cross_row.shape[0] // 2
+    cross_bias = jnp.where(section_at == 0, cross_row[:cross_half], cross_row[cross_half:])
     return (
-        decoded_out,
-        text_out,
-        mel_out,
-        conv_first_grad,
-        conv_bias_grad,
-        conv_second_grad,
-        summed[0][None],
-        summed[1][None],
-        summed[2][None],
-        summed[3][None],
-        summed[4][None],
-        summed[5][None],
-        summed[6][None],
-        summed[7][None],
-        summed[8][None],
-        summed[9][None],
-        cross_bias_out,
+        swap(decoded, 1),
+        swap(text_grad, 1),
+        swap(mel_grad, 1),
+        outs[6],
+        smalls[4],
+        outs[7],
+        smalls[0][None],
+        smalls[1][None],
+        outs[0][None],
+        outs[1][None],
+        outs[2][None],
+        outs[3][None],
+        smalls[2][None],
+        smalls[3][None],
+        outs[4][None],
+        outs[5][None],
+        cross_bias,
     )
 
 

time: 1680 us -> 1050 us (0.62)
  waiting for transfers between devices: 666 us -> 419 us
  other arithmetic: 231 us -> 105 us
  local copies, waits for them, and re-layouts: 272 us -> 149 us
  matrix products: 361 us -> 247 us
  starting transfers between devices: 27.4 us -> 4.46 us
  loops' own time: 22.1 us -> 1.03 us
    ppermute x15 -> x4, waiting for transfers between devices: 403 us -> 1.18 us  [the longest x1 1.18 us: shards(): lax.ppermute(smalls[3][5].astype(jnp.bfloat16), 'section', [(1, 0)])]
    reduce_scatter x0 -> x1, waiting for transfers between devices: none -> 182 us  [shards(): lax.psum_scatter(flat, 'section', scatter_dimension=0, tiled=False)]
    psum x1, waiting for transfers between devices: 249 us -> 101 us  [shards(): flat_all = lax.psum(flat_shard, 'dp').astype(jnp.float32)]
    all_gather x1 -> x7, waiting for transfers between devices: 13.3 us -> 115 us  [the longest x6 115 us: both(): return lax.all_gather(weight, 'section', axis=0, tiled=False)]
    add x24 -> x4, other arithmetic: 75.7 us -> 3.44 us  [the longest x1 1.65 us: self_block_back(): grad + grad_inputs]
    cond x220 -> x0, local copies, waits for them, and re-layouts: 37.5 us -> none
    dot_general x18 -> x15, matrix products: 59.4 us -> 32.1 us  [input_grad(): lax.dot_general(grad_low, weight, (((1,), (1,)), ((), ())), preferred_ele...]
    ppermute x15 -> x4, starting transfers between devices: 27.4 us -> 3.83 us  [the longest x3 2.55 us: swap(): lax.ppermute(send_part, 'section', [(0, 1), (1, 0)]).astype(jnp.float32)]
  transfers between devices with their start and end apart: 17 -> 14, of which waited for: 11 -> 8; matrix products, arithmetic and copies ran while one was open for 2% -> 12% of each run, Pallas kernels for 0% -> 0%
where the time goes in v1:
time: 1050 us; the launch traced here: 1040 us
  waiting for transfers between devices  419 us (40%)
  matrix products  247 us (24%)
  local copies, waits for them, and re-layouts  149 us (14%)
  other arithmetic  105 us (10%)
  blocking collectives  94.8 us (9%)
  between operations  19.8 us (2%)
    reduce_scatter x1, waiting for transfers between devices, shards(): lax.psum_scatter(flat, 'section', scatter_dimension=0, tiled=False)  182 us
    all_gather x6, waiting for transfers between devices, both(): return lax.all_gather(weight, 'section', axis=0, tiled=False)  115 us
    psum x1, waiting for transfers between devices, shards(): flat_all = lax.psum(flat_shard, 'dp').astype(jnp.float32)  101 us
    psum x1, blocking collectives, shards(): lax.psum(lax.psum_scatter(small_flat, 'section', scatter_dimension=0, til...  64.1 us
    dot_general x4, matrix products, one_block(): jnp.einsum('qhd,khd->hqk', grad_block, value_heads, preferred_element_typ...  39.9 us
    dot_general x15, matrix products, matmul(): return jnp.dot(left, right, preferred_element_type=jnp.float32)  39.4 us
    convert_element_type x4, other arithmetic, one_block(): grad_scores = (probability * (grad_prob - jnp.sum(probability * grad_prob...  35.8 us
    dot_general x15, matrix products, weight_grad(): lax.dot_general(inputs, grad_low, (((0,), (0,)), ((), ())), preferred_ele...  35.4 us
  transfers between devices with their start and end apart: 14, of which 8 were waited for; matrix products, arithmetic and copies ran while one was open for 12% of the time, Pallas kernels for 0%

profile of v1, /device:TPU:0, one launch (start us, length us, event | category | flops | bytes accessed | tf_op | source)
XLA Modules:
  0.0 1039.3 jit_solution(11730511139330782560)
XLA Ops:
  12.2 5.3 all_gather.42
  18.1 4.3 all_gather.40
  23.1 4.4 all_gather.39
  29.9 4.2 all-gather
  34.1 7.9 all_gather.44
  50.2 3.6 multiply_convert_fusion.4
  56.6 3.8 fusion.205
  61.1 4.6 all-gather.1
  74.2 14.3 %all-gather.10.cloned.1.call-done = bf16[2,512,1536]{2,1,0:T(8,128)(2,1)} async-done(((bf16[1,512,1536]{2,1,0:T(8,128)(2,1)}), bf16[2,512,1536]{2,1,0:T(8,128)(2,1)}) %all-gather.10.cloned.1.call-update) | async-done | bytes 3145744 | tf_op jit(solution)/shard_map/all_gather | solution.py:551
  112.4 24.2 %while.5 = (s32[]{:T(128)}, bf16[2,512,512]{2,1,0:T(8,128)(2,1)}, f32[2,8,512]{2,1,0:T(8,128)S(1)}, bf16[2,512,8,64]{1,3,2,0:T(8,128)(2,1)S(1)}, bf16[1024,8,64]...) while((s32[]{:T(128)}, bf16[2,512,512]{2,1,0:T(8,128)(2,1)}, f32[2,8,512]{2,1,0:T(8,128)S(1)}, ...), condition=%wide.region_9.10_spmd, body=%wide.region_6.9_spmd.sunk | while | flops 1111748608 | bytes 55705696 | solution.py:192
  118.7 4.9 fusion.304
  127.2 3.4 fusion.303
  130.7 4.9 fusion.304
  136.8 3.6 fusion.214
  146.4 46.0 %all-gather.16.cloned.1.call-done = bf16[2,512,2048]{2,1,0:T(8,128)(2,1)} async-done(((bf16[1,512,2048]{2,1,0:T(8,128)(2,1)}), bf16[2,512,2048]{2,1,0:T(8,128)(2,1)}) %all-gather.16.cloned.1.call-update) | async-done | bytes 4194320 | tf_op jit(solution)/shard_map/all_gather | solution.py:551
  192.3 7.8 multiply_convert_fusion.2
  200.2 50.3 %all-gather.18.cloned.1.call-done = bf16[2,2048,512]{2,1,0:T(8,128)(2,1)} async-done(((bf16[1,2048,512]{2,1,0:T(8,128)(2,1)}), bf16[2,2048,512]{2,1,0:T(8,128)(2,1)}) %all-gather.18.cloned.1.call-update) | async-done | bytes 4194320 | tf_op jit(solution)/shard_map/all_gather | solution.py:551
  250.5 5.2 fusion.215
  260.9 5.1 copy-done.4
  269.3 4.1 all-gather.20.cloned.1.call-done
  275.6 7.5 fusion.90
  294.3 13.9 %multiply_reduce_fusion.2 = (f32[8,448]{1,0:T(8,128)S(1)}, f32[8,448,1024]{2,1,0:T(8,128)}) fusion(f32[8,448,1024]{2,1,0:T(8,128)} %copy-done.4, f32[8,448]{1,0:T(8,128)S(1)} %log_add_fusion.1, bf16[448,8,64]{0,2,1:T(8,128)(2,1)S(1)} %bitcast.522, bf16[1024,8,64]{0,2,1:T(8,128)(2,1)} %bitcast.542), kind=kOutput, calls=%fused_computation.41 | convolution fusion | flops 484438528 | bytes 30896128 | tf_op jit(solution)/shard_map/while/body/eval_jaxpr/qhd,khd->hqk/dot_general | solution.py:213
  308.2 7.7 multiply_convert_fusion.1
  326.9 6.0 fusion.208
  332.9 4.6 multiply_reduce_fusion.4
  337.5 7.4 multiply_convert_fusion.3
  349.0 4.7 multiply_convert_fusion.6
  353.8 3.8 convert_reduce_fusion
  371.7 3.8 fusion.56
  376.8 6.4 fusion.221
  383.2 3.9 convolution_convert_fusion.1
  387.1 4.3 fusion.218
  402.5 4.0 reshape.790
  409.9 94.1 %while.6 = (s32[]{:T(128)}, f32[1024,8,64]{0,2,1:T(8,128)}, f32[1024,8,64]{0,2,1:T(8,128)}, f32[2,512,512]{1,2,0:T(8,128)}, bf16[2,512,8,64]{1,3,2,0:T(8,128)(2,...) while((s32[]{:T(128)}, f32[1024,8,64]{0,2,1:T(8,128)}, ...), condition=%wide.region_34.35_spmd.clone, body=%wide.region_32.34_spmd.clone.sunk | while | flops 2737565696 | bytes 310493504 | solution.py:239
  412.7 10.7 %multiply_reduce_fusion.29 = (f32[8,512]{1,0:T(8,128)S(1)}, f32[8,512,1024]{2,1,0:T(8,128)}) fusion(f32[8,512,1024]{2,1,0:T(8,128)S(1)} %fusion.314, f32[8,512]{1,0:T(8,128)S(1)} %dynamic-slice_bitcast_fusion.2, bf16[1024,8,64]{0,2,1:T(8,128)(2,1)} %get-tuple-element.607, bf16[2,512,8,64]{1,3,2,0:T(8,128)(2,1)} %get-tuple-element.606, s32[]{:T(128)S(6)} %copy.214), kind=kOutput, calls=%fused_computation.14.clone.1 | convolution fusion | flops 553644032 | bytes 35160068 | tf_op jit(solution)/shard_map/while/body/eval_jaxpr/qhd,khd->hqk/dot_general | solution.py:213
  423.8 10.4 multiply_convert_fusion.8
  434.2 6.5 bitcast_add_fusion.4
  443.7 4.8 bitcast_add_fusion.5
  448.5 6.8 convolution_multiply_fusion.5
  459.2 10.7 %multiply_reduce_fusion.29 = (f32[8,512]{1,0:T(8,128)S(1)}, f32[8,512,1024]{2,1,0:T(8,128)}) fusion(f32[8,512,1024]{2,1,0:T(8,128)S(1)} %fusion.314, f32[8,512]{1,0:T(8,128)S(1)} %dynamic-slice_bitcast_fusion.2, bf16[1024,8,64]{0,2,1:T(8,128)(2,1)} %get-tuple-element.607, bf16[2,512,8,64]{1,3,2,0:T(8,128)(2,1)} %get-tuple-element.606, s32[]{:T(128)S(6)} %copy.214), kind=kOutput, calls=%fused_computation.14.clone.1 | convolution fusion | flops 553644032 | bytes 35160068 | tf_op jit(solution)/shard_map/while/body/eval_jaxpr/qhd,khd->hqk/dot_general | solution.py:213
  470.4 10.4 multiply_convert_fusion.8
  480.7 7.1 bitcast_add_fusion.4
  490.8 4.8 bitcast_add_fusion.5
  495.6 6.8 convolution_multiply_fusion.5
  511.5 4.8 convolution_convert_fusion.5
  516.3 3.7 fusion.219
  532.4 5.2 copy.164
  537.7 6.1 reshape.746
  543.8 5.1 fusion.194
  557.9 3.7 stack.322
  561.5 3.7 stack.321
  565.2 4.3 stack.328
  569.6 4.3 stack.327
  573.9 4.3 fusion.55
  592.6 7.6 pad.31
  612.6 181.9 %reduce-scatter.2.cloned.1.call-done = bf16[1,8192,512]{2,1,0:T(8,128)(2,1)} async-done(((bf16[2,8192,512]{2,1,0:T(8,128)(2,1)}), bf16[1,8192,512]{2,1,0:T(8,128)(2,1)}) %reduce-scatter.2.cloned.1.call-update) | async-done | bytes 8388624 | tf_op jit(solution)/shard_map/reduce_scatter | solution.py:599
  802.3 16.0 %all-reduce.12.cloned.1.call-done = f32[2,8448]{1,0:T(2,128)} async-done(((f32[2,8448]{1,0:T(2,128)}), f32[2,8448]{1,0:T(2,128)}) %all-reduce.12.cloned.1.call-update) | async-done | bytes 67600
  820.0 64.1 %psum.15 = f32[8448]{0:T(1024)S(1)} all-reduce(f32[8448]{0:T(1024)S(1)} %dynamic-slice_reduce_fusion), channel_id=1, replica_groups=mesh['section'=2,'dp'=16] {'dp'}, use_global_device_ids=true, to_apply=%region_67.68 | all-reduce | flops 8448 | bytes 67584 | tf_op jit(solution)/shard_map/psum | solution.py:604
  893.1 100.6 %all-reduce.10.cloned.1.call-done = bf16[8192,512]{1,0:T(8,128)(2,1)} async-done(((bf16[8192,512]{1,0:T(8,128)(2,1)}), bf16[8192,512]{1,0:T(8,128)(2,1)}) %all-reduce.10.cloned.1.call-update) | async-done | bytes 8388624 | tf_op jit(solution)/shard_map/psum | solution.py:602
  993.7 11.6 %convert_element_type.630 = f32[8192,512]{1,0:T(8,128)} convert(bf16[8192,512]{1,0:T(8,128)(2,1)} %all-reduce.10.cloned.1.call-done) | non-fusion elementwise | flops 4194304 | bytes 25165824 | tf_op jit(solution)/shard_map/convert_element_type | solution.py:602
  1005.4 3.6 slice_bitcast_fusion.27
  1009.0 4.6 slice_bitcast_fusion
  1022.1 4.2 slice.501
  1026.4 5.6 broadcast_in_dim_reshape.18
  (697 shorter events, 228.3 us)
Async XLA Ops:
  7.2 60.9 %all-gather.14.cloned.1.call-start = ((), (), s32[]{:S(2)}) async-start(), calls=%async_computation.3 | async-start | bytes 2359296 | tf_op jit(solution)/shard_map/all_gather | solution.py:558
  7.9 80.6 %all-gather.10.cloned.1.call-start = ((), (), s32[]{:S(2)}) async-start(), calls=%async_computation.1 | async-start | bytes 4718592 | tf_op jit(solution)/shard_map/all_gather | solution.py:551
  8.7 128.0 %all-gather.12.cloned.1.call-start = ((), (), s32[]{:S(2)}) async-start(), calls=%async_computation.2 | async-start | bytes 1572864 | tf_op jit(solution)/shard_map/all_gather | solution.py:551
  9.4 8.7 copy-start.162
  9.4 13.6 %copy-start.163 = (bf16[1,3,512]{2,1,0:T(4,128)(2,1)S(1)}, bf16[1,3,512]{2,1,0:T(4,128)(2,1)}, u32[]{:S(2)}) copy-start(bf16[1,3,512]{2,1,0:T(4,128)(2,1)} %param.38) | copy-start | bytes 9220
  9.4 18.6 %copy-start.76 = (bf16[2,448,512]{2,1,0:T(8,128)(2,1)S(1)}, bf16[2,448,512]{2,1,0:T(8,128)(2,1)}, u32[]{:S(2)}) copy-start(bf16[2,448,512]{2,1,0:T(8,128)(2,1)} %param.32) | copy-start | bytes 2752516
  9.5 132.3 %all-gather.22.cloned.1.call-start = ((), (), s32[]{:S(2)}) async-start(), calls=%async_computation.7 | async-start | bytes 1572864 | tf_op jit(solution)/shard_map/all_gather | solution.py:551
  10.0 18.5 %copy-start.83 = (bf16[1024,512]{1,0:T(8,128)(2,1)S(1)}, bf16[1024,512]{1,0:T(8,128)(2,1)}, u32[]{:S(2)}) copy-start(bf16[1024,512]{1,0:T(8,128)(2,1)} %param.34) | copy-start | bytes 3145732
  10.0 182.3 %all-gather.16.cloned.1.call-start = ((), (), s32[]{:S(2)}) async-start(), calls=%async_computation.4 | async-start | bytes 6291456 | tf_op jit(solution)/shard_map/all_gather | solution.py:551
  10.6 19.3 %copy-start.192 = (bf16[256]{0:T(256)(128)(2,1)S(1)}, bf16[256]{0:T(256)(128)(2,1)}, u32[]{:S(2)}) copy-start(bf16[256]{0:T(256)(128)(2,1)} %param.36) | copy-start | bytes 1540
  10.6 23.5 %copy-start.111 = (bf16[3,80,256]{2,1,0:T(8,128)(2,1)S(1)}, bf16[3,80,256]{2,1,0:T(8,128)(2,1)}, u32[]{:S(2)}) copy-start(bf16[3,80,256]{2,1,0:T(8,128)(2,1)} %param.35) | copy-start | bytes 368644
  10.6 31.4 %copy-start.193 = (s32[2]{0:T(128)S(1)}, s32[2]{0:T(128)}, u32[]{:S(2)}) copy-start(s32[2]{0:T(128)} %param.27) | copy-start | bytes 28
  10.7 31.9 %copy-start.194 = (s32[2]{0:T(128)S(1)}, s32[2]{0:T(128)}, u32[]{:S(2)}) copy-start(s32[2]{0:T(128)} %param.28) | copy-start | bytes 28
  10.7 34.5 %copy-start.195 = (s32[2]{0:T(128)S(1)}, s32[2]{0:T(128)}, u32[]{:S(2)}) copy-start(s32[2]{0:T(128)} %param.29) | copy-start | bytes 28
  10.7 35.1 %copy-start.196 = (s32[2]{0:T(128)S(1)}, s32[2]{0:T(128)}, u32[]{:S(2)}) copy-start(s32[2]{0:T(128)} %param.30) | copy-start | bytes 28
  10.7 37.6 %copy-start.88 = (bf16[2,80,2048]{2,1,0:T(8,128)(2,1)S(1)}, bf16[2,80,2048]{2,1,0:T(8,128)(2,1)}, u32[]{:S(2)}) copy-start(bf16[2,80,2048]{2,1,0:T(8,128)(2,1)} %param.26) | copy-start | bytes 1966084
  10.7 239.8 %all-gather.18.cloned.1.call-start = ((), (), s32[]{:S(2)}) async-start(), calls=%async_computation.5 | async-start | bytes 6291456 | tf_op jit(solution)/shard_map/all_gather | solution.py:551
  11.3 262.1 %all-gather.20.cloned.1.call-start = ((), (), s32[]{:S(2)}) async-start(), calls=%async_computation.6 | async-start | bytes 1572864 | tf_op jit(solution)/shard_map/all_gather | solution.py:551
  12.0 782.4 %reduce-scatter.2.cloned.1.call-start = ((), (), s32[]{:S(2)}) async-start(), calls=%async_computation.8 | async-start | bytes 25165824 | tf_op jit(solution)/shard_map/reduce_scatter | solution.py:599
  23.1 65.5 %copy-start.165 = (f32[1,1,512]{2,1,0:T(1,128)}, f32[1,1,512]{2,1,0:T(1,128)S(1)}, u32[]{:S(2)}) copy-start(f32[1,1,512]{2,1,0:T(1,128)S(1)} %get-tuple-element.403) | copy-start | bytes 6148
  23.1 77.8 %copy-start.167 = (f32[1,1,512]{2,1,0:T(1,128)}, f32[1,1,512]{2,1,0:T(1,128)S(1)}, u32[]{:S(2)}) copy-start(f32[1,1,512]{2,1,0:T(1,128)S(1)} %get-tuple-element.402) | copy-start | bytes 6148
  28.1 60.4 %copy-start.136 = (f32[1,1,512]{2,1,0:T(1,128)}, f32[1,1,512]{2,1,0:T(1,128)S(1)}, u32[]{:S(2)}) copy-start(f32[1,1,512]{2,1,0:T(1,128)S(1)} %get-tuple-element.397) | copy-start | bytes 6148
  28.1 72.7 %copy-start.121 = (f32[1,1,512]{2,1,0:T(1,128)}, f32[1,1,512]{2,1,0:T(1,128)S(1)}, u32[]{:S(2)}) copy-start(f32[1,1,512]{2,1,0:T(1,128)S(1)} %get-tuple-element.396) | copy-start | bytes 6148
  28.3 60.3 %copy-start.123 = (f32[448]{0:T(512)}, f32[448]{0:T(512)S(1)}, u32[]{:S(2)}) copy-start(f32[448]{0:T(512)S(1)} %broadcast_multiply_fusion.17) | copy-start | bytes 5380
  28.6 60.0 %copy-start.142 = (f32[448]{0:T(512)}, f32[448]{0:T(512)S(1)}, u32[]{:S(2)}) copy-start(f32[448]{0:T(512)S(1)} %add_rsqrt_fusion.5) | copy-start | bytes 5380
  42.0 8.1 copy-start.65
  60.4 9.6 copy-start.52
  60.7 10.1 copy-start.31
  73.9 26.9 %copy-start.12 = (f32[1024,512]{0,1:T(8,128)}, f32[1024,512]{0,1:T(8,128)S(1)}, u32[]{:S(2)}) copy-start(f32[1024,512]{0,1:T(8,128)S(1)} %get-tuple-element.347) | copy-start | bytes 6291460
  73.9 26.9 %copy-start.113 = (f32[1024]{0:T(1024)}, f32[1024]{0:T(1024)S(1)}, u32[]{:S(2)}) copy-start(f32[1024]{0:T(1024)S(1)} %broadcast_multiply_fusion.8) | copy-start | bytes 12292
  74.2 26.6 %copy-start.115 = (f32[1024]{0:T(1024)}, f32[1024]{0:T(1024)S(1)}, u32[]{:S(2)}) copy-start(f32[1024]{0:T(1024)S(1)} %add_rsqrt_fusion.2) | copy-start | bytes 12292
  112.4 24.3 %copy-start.141 = (f32[1,1,512]{2,1,0:T(1,128)S(1)}, f32[1,1,512]{2,1,0:T(1,128)}, u32[]{:S(2)}) copy-start(f32[1,1,512]{2,1,0:T(1,128)} %get-tuple-element.383) | copy-start | bytes 6148
  141.3 177.6 %copy-start.39 = (f32[448,512]{1,0:T(8,128)}, f32[448,512]{1,0:T(8,128)S(1)}, u32[]{:S(2)}) copy-start(f32[448,512]{1,0:T(8,128)S(1)} %get-tuple-element.418) | copy-start | bytes 2752516
  141.3 51.0 %copy-start.127 = (f32[1,1,512]{2,1,0:T(1,128)S(1)}, f32[1,1,512]{2,1,0:T(1,128)}, u32[]{:S(2)}) copy-start(f32[1,1,512]{2,1,0:T(1,128)} %get-tuple-element.395) | copy-start | bytes 6148
  141.4 58.8 %copy-start.125 = (f32[448]{0:T(512)}, f32[448]{0:T(512)S(1)}, u32[]{:S(2)}) copy-start(f32[448]{0:T(512)S(1)} %broadcast_multiply_fusion.16) | copy-start | bytes 5380
  141.8 50.6 %copy-start.15 = (f32[1024,512]{0,1:T(8,128)S(1)}, f32[1024,512]{0,1:T(8,128)}, u32[]{:S(2)}) copy-start(f32[1024,512]{0,1:T(8,128)} %copy-done.14) | copy-start | bytes 6291460
  146.3 112.4 %copy-start.44 = (bf16[448,512]{0,1:T(8,128)(2,1)}, bf16[448,512]{0,1:T(8,128)(2,1)S(1)}, u32[]{:S(2)}) copy-start(bf16[448,512]{0,1:T(8,128)(2,1)S(1)} %copy.148) | copy-start | bytes 1376260
  275.5 7.6 copy-start.82
  275.5 7.6 copy-start.63
  275.5 7.6 copy-start.155
  275.5 8.4 copy-start.187
  283.7 7.9 copy-start.41
  294.3 13.9 %copy-start.50 = (bf16[448,512]{0,1:T(8,128)(2,1)}, bf16[448,512]{0,1:T(8,128)(2,1)S(1)}, u32[]{:S(2)}) copy-start(bf16[448,512]{0,1:T(8,128)(2,1)S(1)} %copy.149) | copy-start | bytes 1376260
  294.3 13.9 %slice-start = ((s8[14680064]{0:T(1024)(128)(4,1)}), s8[4194304]{0:T(1024)(128)(4,1)S(1)}, s32[]{:S(2)}) async-start(s8[14680064]{0:T(1024)(128)(4,1)} %bitcast.503), calls=%async_computation.11 | async-start | bytes 8388608
  294.3 13.9 %slice-start.1 = ((s8[14680064]{0:T(1024)(128)(4,1)}), s8[4194304]{0:T(1024)(128)(4,1)S(1)}, s32[]{:S(2)}) async-start(s8[14680064]{0:T(1024)(128)(4,1)} %bitcast.503), calls=%async_computation.12 | async-start | bytes 8388608
  294.3 13.9 %slice-start.2 = ((s8[14680064]{0:T(1024)(128)(4,1)}), s8[4194304]{0:T(1024)(128)(4,1)S(1)}, s32[]{:S(2)}) async-start(s8[14680064]{0:T(1024)(128)(4,1)} %bitcast.503), calls=%async_computation.13 | async-start | bytes 8388608
  294.3 13.9 %slice-start.3 = ((s8[14680064]{0:T(1024)(128)(4,1)}), s8[2097152]{0:T(1024)(128)(4,1)S(1)}, s32[]{:S(2)}) async-start(s8[14680064]{0:T(1024)(128)(4,1)} %bitcast.503), calls=%async_computation.14 | async-start | bytes 4194304
  320.4 12.5 %slice-start.8 = ((s8[7340032]{0:T(1024)(128)(4,1)}), s8[3145728]{0:T(1024)(128)(4,1)S(1)}, s32[]{:S(2)}) async-start(s8[7340032]{0:T(1024)(128)(4,1)} %bitcast.507), calls=%async_computation.19 | async-start | bytes 6291456
  337.4 7.4 copy-start.49
  337.5 16.2 %slice-start.4 = ((s8[14680064]{0:T(1024)(128)(4,1)}), s8[2097152]{0:T(1024)(128)(4,1)S(1)}, s32[]{:S(2)}) async-start(s8[14680064]{0:T(1024)(128)(4,1)} %bitcast.505), calls=%async_computation.15 | async-start | bytes 4194304
  337.5 16.2 %slice-start.5 = ((s8[14680064]{0:T(1024)(128)(4,1)}), s8[4194304]{0:T(1024)(128)(4,1)S(1)}, s32[]{:S(2)}) async-start(s8[14680064]{0:T(1024)(128)(4,1)} %bitcast.505), calls=%async_computation.16 | async-start | bytes 8388608
  344.9 8.8 slice-start.6
  412.7 11.2 %copy-start = (f32[8,512,1024]{2,1,0:T(8,128)}, f32[8,512,1024]{2,1,0:T(8,128)S(1)}, u32[]{:S(2)}) copy-start(f32[8,512,1024]{2,1,0:T(8,128)S(1)} %fusion.314) | copy-start | bytes 50331652 | tf_op jit(solution)/shard_map/while
  434.2 8.9 copy-start.1
  434.2 9.5 copy-start.10
  459.2 11.2 %copy-start = (f32[8,512,1024]{2,1,0:T(8,128)}, f32[8,512,1024]{2,1,0:T(8,128)S(1)}, u32[]{:S(2)}) copy-start(f32[8,512,1024]{2,1,0:T(8,128)S(1)} %fusion.314) | copy-start | bytes 50331652 | tf_op jit(solution)/shard_map/while
  480.7 9.5 copy-start.1
  480.7 10.1 copy-start.10
  600.3 218.1 %all-reduce.12.cloned.1.call-start = ((), (), s32[]{:S(2)}) async-start(), calls=%async_computation.10 | async-start | bytes 135168
  606.1 284.9 %collective-permute-start = (bf16[448,256]{1,0:T(8,128)(2,1)S(1)}, bf16[448,256]{1,0:T(8,128)(2,1)S(1)}, u32[]{:S(2)}, u32[]{:S(2)}) collective-permute-start(bf16[448,256]{1,0:T(8,128)(2,1)S(1)} %select_convert_fusion.1), channel_id=1, source_target_pairs={{0,16},{16,0},{1,17},{17,1},{2,18},{18,2},{3,19},{19,3},{4,20},{20... | collective-permute-start | bytes 688136 | tf_op jit(solution)/shard_map/ppermute | solution.py:625
  612.5 381.2 %all-reduce.10.cloned.1.call-start = ((), (), s32[]{:S(2)}) async-start(), calls=%async_computation.9 | async-start | bytes 16777216 | tf_op jit(solution)/shard_map/psum | solution.py:602
  797.4 94.7 %collective-permute-start.1 = (bf16[448,256]{1,0:T(8,128)(2,1)S(1)}, bf16[448,256]{1,0:T(8,128)(2,1)S(1)}, u32[]{:S(2)}, u32[]{:S(2)}) collective-permute-start(bf16[448,256]{1,0:T(8,128)(2,1)S(1)} %select_convert_fusion), channel_id=1, source_target_pairs={{0,16},{16,0},{1,17},{17,1},{2,18},{18,2},{3,19},{19,3},{4,20},{20... | collective-permute-start | bytes 688136 | tf_op jit(solution)/shard_map/ppermute | solution.py:625
  800.4 89.7 %collective-permute-start.2 = (bf16[80,1024]{1,0:T(8,128)(2,1)S(1)}, bf16[80,1024]{1,0:T(8,128)(2,1)S(1)}, u32[]{:S(2)}, u32[]{:S(2)}) collective-permute-start(bf16[80,1024]{1,0:T(8,128)(2,1)S(1)} %select_convert_fusion.2), channel_id=1, source_target_pairs={{0,16},{16,0},{1,17},{17,1},{2,18},{18,2},{3,19},{19,3},{4,20},{20... | collective-permute-start | bytes 491528 | tf_op jit(solution)/shard_map/ppermute | solution.py:625
  884.1 5.5 collective-permute-start.3
  (170 other events, 571.0 us)
Sparse Core Ops, SparseCore 0:
  9.6 32.5 all-gather.13
  43.7 44.7 all-gather.9
  90.1 21.2 all-gather.11
  112.8 21.2 all-gather.21
  135.5 56.7 all-gather.15
  193.7 56.7 all-gather.17
  252.1 21.2 all-gather.19
  600.4 194.0 reduce-scatter.1
  797.4 20.9 all-reduce.11
  822.4 171.2 all-reduce.9

commit v2 on v1

v2 whole, which is shorter than its diff:
```python
import functools

import jax
import jax.numpy as jnp
from jax import lax
from jax.experimental import pallas as pl
from jax.experimental.pallas import tpu as pltpu
from jax.sharding import PartitionSpec as P

HEADS = 8
epsilon = 1e-05
root_half = 0.7071067811865476
gauss_norm = 0.3989422804014327
log2_e = 1.4426950408889634
VMEM_BYTES = 56 << 20

f32 = jnp.float32
low = jnp.bfloat16


def dot(left, right):
    return lax.dot_general(left, right, (((1,), (0,)), ((), ())), preferred_element_type=f32)


def dot_t(left, right):
    return lax.dot_general(left, right, (((1,), (1,)), ((), ())), preferred_element_type=f32)


def dot_tt(left, right):
    return lax.dot_general(left, right, (((0,), (0,)), ((), ())), preferred_element_type=f32)


def gelu_both(inputs):
    ratio = 1.0 / (1.0 + (0.3275911 * root_half) * jnp.abs(inputs))
    bell = jnp.exp2((-0.5 * log2_e) * inputs * inputs)
    tail = ratio * (
        0.127414796
        + ratio * (-0.142248368 + ratio * (0.7107068705 + ratio * (-0.7265760135 + ratio * 0.5307027145)))
    )
    tail = tail * bell
    below = jnp.where(inputs >= 0.0, 1.0 - tail, tail)
    return inputs * below, below + inputs * bell * gauss_norm


def norm_rows(inputs):
    centred = inputs - jnp.mean(inputs, axis=-1, keepdims=True)
    inverse = lax.rsqrt(jnp.mean(centred * centred, axis=-1, keepdims=True) + epsilon)
    return centred * inverse, inverse


def norm_back(grad, gain, normed, inverse):
    scaled = grad * gain
    return inverse * (
        scaled
        - jnp.mean(scaled, axis=-1, keepdims=True)
        - normed * jnp.mean(scaled * normed, axis=-1, keepdims=True)
    )


def col_sum(inputs):
    return jnp.sum(inputs, axis=0, keepdims=True)


class Side:
    def __init__(self, side, own, other):
        self.side, self.own, self.other = side, own, other


def call(body, name, steps, block, ins, outs, scratch=(), reverse=False, flops=0, grid=None):
    arrays, specs, kinds, weight_scratch = [], [], [], []
    at = (lambda i: steps - 1 - i) if reverse else (lambda i: i)
    for array, kind in ins:
        if kind == "side":
            arrays += [array.own, array.other]
            specs += [pl.BlockSpec(memory_space=pl.ANY)] * 2
            weight_scratch.append(pltpu.VMEM(array.own.shape[1:], array.own.dtype))
        elif kind == "rows":
            arrays.append(array)
            specs.append(pl.BlockSpec((block, array.shape[1]), lambda i: (at(i), 0)))
        elif kind == "smem":
            arrays.append(array)
            specs.append(pl.BlockSpec(memory_space=pltpu.SMEM))
        else:
            arrays.append(array)
            specs.append(
                pl.BlockSpec(
                    array.shape,
                    lambda i, n=array.ndim: (0,) * n,
                    pipeline_mode=pl.Buffered(1),
                )
            )
        kinds.append((kind, array.side if kind == "side" else None))
    out_specs = [
        pl.BlockSpec((block, shape[1]), lambda i: (at(i), 0))
        if kind == "rows"
        else pl.BlockSpec(shape, lambda i, n=len(shape): (0,) * n)
        for shape, dtype, kind in outs
    ]
    n_in, n_out, n_weight = len(arrays), len(outs), len(weight_scratch)

    def kernel(*refs):
        in_refs, out_refs = refs[:n_in], refs[n_in : n_in + n_out]
        weights = refs[n_in + n_out : n_in + n_out + n_weight]
        extra = refs[n_in + n_out + n_weight :]
        given, r, w, loads = [], 0, 0, []
        for kind, side in kinds:
            if kind == "side":
                loads.append((side, in_refs[r], in_refs[r + 1], weights[w]))
                given.append(weights[w])
                r, w = r + 2, w + 1
            else:
                given.append(in_refs[r])
                r += 1
        step = pl.program_id(0)
        if loads:
            sem = extra[-1]
            extra = extra[:-1]

            @pl.when(step == 0)
            def _():
                mine = lax.axis_index("section")
                for n, (side, own, other, held) in enumerate(loads):

                    @pl.when(mine == side)
                    def _(own=own, held=held, n=n):
                        pltpu.make_async_copy(own.at[0], held, sem.at[n]).start()

                    @pl.when(mine != side)
                    def _(other=other, held=held, n=n):
                        pltpu.make_async_copy(other.at[0], held, sem.at[n]).start()

                for n, (side, own, other, held) in enumerate(loads):
                    pltpu.make_async_copy(own.at[0], held, sem.at[n]).wait()

        for ref, (shape, dtype, kind) in zip(out_refs, outs):
            if kind == "sums":

                @pl.when(step == 0)
                def _(ref=ref):
                    ref[...] = jnp.zeros(ref.shape, ref.dtype)

        body(step, given, out_refs, extra)

    scratch_shapes = weight_scratch + list(scratch)
    if weight_scratch:
        scratch_shapes.append(pltpu.SemaphoreType.DMA((n_weight,)))
    total = sum(a.size * a.dtype.itemsize for a in arrays) + sum(
        2 * s[0] * s[1] for s, d, k in outs
    )
    return pl.pallas_call(
        kernel,
        name=name,
        grid=(steps,),
        in_specs=specs,
        out_specs=out_specs,
        out_shape=[jax.ShapeDtypeStruct(shape, dtype) for shape, dtype, kind in outs],
        scratch_shapes=scratch_shapes,
        compiler_params=pltpu.CompilerParams(
            dimension_semantics=("arbitrary",), vmem_limit_bytes=VMEM_BYTES
        ),
        cost_estimate=pl.CostEstimate(flops=int(flops), bytes_accessed=int(total), transcendentals=0),
    )(*arrays)


def row(ref, n):
    return ref[n : n + 1, :].astype(f32)


def stem(taps, weight, bias, second, smalls, positions):
    rows, width = positions.shape
    block = 256

    def body(step, given, outs, extra):
        taps, weight, bias, second, smalls, positions = given
        encoded, even_out, odd_out, even_slope, odd_slope, slope_out = outs
        (carry,) = extra

        @pl.when(step == 0)
        def _():
            carry[...] = jnp.zeros(carry.shape, f32)

        pre = dot(taps[:, 0:384], weight[...]) + bias[...].astype(f32)
        value, slope = gelu_both(pre)
        even = value.astype(low)
        even_out[...] = even
        even_slope[...] = slope.astype(low)
        pre = dot(taps[:, 128:512], weight[...]) + bias[...].astype(f32)
        value, slope = gelu_both(pre)
        odd = value.astype(low)
        odd_out[...] = odd
        odd_slope[...] = slope.astype(low)
        prior = dot(odd, second[0])
        moved = pltpu.roll(prior, 1, 0)
        at_row = lax.broadcasted_iota(jnp.int32, (block, width), 0)
        moved = jnp.where(at_row == 0, carry[0:1, :], moved)
        carry[0:1, :] = prior[block - 1 : block, :]
        pre = moved + dot(even, second[1]) + dot(odd, second[2]) + row(smalls, 10)
        value, slope = gelu_both(pre)
        slope_out[...] = slope.astype(low)
        encoded[...] = value + positions[...].astype(f32)

    shape = (rows, width)
    return call(
        body, "stem", rows // block, block,
        [(taps, "rows"), (weight, "full"), (bias, "full"), (second, "full"), (smalls, "full"), (positions, "rows")],
        [(shape, f32, "rows")] + [(shape, low, "rows")] * 5,
        scratch=[pltpu.VMEM((8, width), f32)],
        flops=2 * rows * width * (768 + 3 * width),
    )


def project(inputs, weight, smalls, block):
    rows, width = inputs.shape

    def body(step, given, outs, extra):
        inputs, weight, smalls = given
        low_out, joint_out = outs
        normed, inverse = norm_rows(inputs[...].astype(f32))
        rounded = (normed * row(smalls, 0) + row(smalls, 3)).astype(low)
        low_out[...] = rounded
        part = dot(rounded, weight[:, :width])
        joint_out[:, :width] = (part + row(smalls, 6)).astype(low) * 0.125
        joint_out[:, width : 2 * width] = dot(rounded, weight[:, width : 2 * width]).astype(low)
        part = dot(rounded, weight[:, 2 * width :])
        joint_out[:, 2 * width :] = (part + row(smalls, 7)).astype(low)

    return call(
        body, "project", rows // block, block,
        [(inputs, "rows"), (weight, "side"), (smalls, "full")],
        [((rows, width), low, "rows"), ((rows, 3 * width), low, "rows")],
        flops=6 * rows * width * width,
    )


def attend(queries, keys, values, cols, causal, block):
    rows, key_rows = queries.shape[0], keys.shape[0]
    pairs, steps = HEADS // 2, rows // block

    def kernel(query_ref, key_ref, value_ref, mixed_ref, log_ref):
        lane = lax.broadcasted_iota(jnp.int32, (1, 128), 1)
        query, key, value = query_ref[...], key_ref[...], value_ref[...]
        mixed, logs = [], []
        for head in range(2):
            part = jnp.where(lane // 64 == head, query, jnp.zeros_like(query))
            scores = dot_t(part, key)
            if causal:
                key_at = lax.broadcasted_iota(jnp.int32, scores.shape, 1)
                query_at = lax.broadcasted_iota(jnp.int32, scores.shape, 0) + pl.program_id(1) * block
                scores = jnp.where(key_at <= query_at, scores, -1e30)
            top = jnp.max(scores, axis=1, keepdims=True) * log2_e
            exponent = jnp.exp2(scores * log2_e - top)
            total = jnp.sum(exponent, axis=1, keepdims=True)
            mixed.append(dot(exponent.astype(low), value) * (1.0 / total))
            logs.append(top + jnp.log2(total))
        mixed_ref[...] = jnp.where(lane < 64, mixed[0], mixed[1]).astype(low)
        both = jnp.where(lane == 0, logs[0], logs[1])
        log_ref[...] = both.T[0:8, :]

    q_at, k_at, v_at = cols
    return pl.pallas_call(
        kernel,
        name="attend",
        grid=(pairs, steps),
        in_specs=[
            pl.BlockSpec((block, 128), lambda h, i: (i, q_at + h)),
            pl.BlockSpec((key_rows, 128), lambda h, i: (0, k_at + h)),
            pl.BlockSpec((key_rows, 128), lambda h, i: (0, v_at + h)),
        ],
        out_specs=[
            pl.BlockSpec((block, 128), lambda h, i: (i, h)),
            pl.BlockSpec((8, block), lambda h, i: (h, i)),
        ],
        out_shape=[
            jax.ShapeDtypeStruct((rows, 128 * pairs), low),
            jax.ShapeDtypeStruct((8 * pairs, rows), f32),
        ],
        compiler_params=pltpu.CompilerParams(
            dimension_semantics=("arbitrary", "arbitrary"), vmem_limit_bytes=VMEM_BYTES
        ),
        cost_estimate=pl.CostEstimate(
            flops=16 * rows * key_rows * 512, bytes_accessed=2 * 512 * (2 * rows + 2 * key_rows), transcendentals=0
        ),
    )(queries, keys, values)


def attend_back(queries, keys, values, cols, logs, grad, causal, round_sums, block):
    rows, key_rows = queries.shape[0], keys.shape[0]
    pairs, steps = HEADS // 2, rows // block

    def kernel(
        query_ref, key_ref, value_ref, log_ref, grad_ref,
        query_out, key_out, value_out, sum_out, key_acc, value_acc, key_turned,
    ):
        step = pl.program_id(1)
        lane = lax.broadcasted_iota(jnp.int32, (1, 128), 1)

        @pl.when(step == 0)
        def _():
            key_acc[...] = jnp.zeros(key_acc.shape, f32)
            value_acc[...] = jnp.zeros(value_acc.shape, f32)
            sum_out[...] = jnp.zeros(sum_out.shape, f32)
            key_turned[...] = key_ref[...].astype(f32).T.astype(low)

        query, key, value, grad = query_ref[...], key_ref[...], value_ref[...], grad_ref[...]
        turned = key_turned[...]
        sub = lax.broadcasted_iota(jnp.int32, (128, 1), 0)
        query_turned = jnp.zeros((128, block), f32)
        for head in range(2):
            part = jnp.where(lane // 64 == head, query, jnp.zeros_like(query))
            grad_part = jnp.where(lane // 64 == head, grad, jnp.zeros_like(grad))
            scores = dot_t(key, part)
            chance = jnp.exp2(scores * log2_e - log_ref[head : head + 1, :])
            if causal:
                key_at = lax.broadcasted_iota(jnp.int32, scores.shape, 0)
                query_at = lax.broadcasted_iota(jnp.int32, scores.shape, 1) + step * block
                chance = jnp.where(key_at <= query_at, chance, 0.0)
            grad_chance = dot_t(value, grad_part)
            product = chance * grad_chance
            grad_scores = (product - chance * jnp.sum(product, axis=0, keepdims=True)).astype(low)
            value_acc[...] += dot(chance.astype(low), grad_part)
            key_acc[...] += dot(grad_scores, part)
            query_turned += dot(jnp.where(sub // 64 == head, turned, jnp.zeros_like(turned)), grad_scores)
        grad_query = query_turned.T * 0.125
        query_out[...] = grad_query.astype(low)
        sum_out[0:1, :] += col_sum(grad_query)

        @pl.when(step == steps - 1)
        def _():
            key_out[...] = key_acc[...].astype(low)
            rounded = value_acc[...].astype(low)
            value_out[...] = rounded
            sum_out[1:2, :] = col_sum(rounded.astype(f32) if round_sums else value_acc[...])

    q_at, k_at, v_at = cols
    row_spec = pl.BlockSpec((block, 128), lambda h, i: (i, h))
    key_spec = pl.BlockSpec((key_rows, 128), lambda h, i: (0, h))
    return pl.pallas_call(
        kernel,
        name="attend_back",
        grid=(pairs, steps),
        in_specs=[
            pl.BlockSpec((block, 128), lambda h, i: (i, q_at + h)),
            pl.BlockSpec((key_rows, 128), lambda h, i: (0, k_at + h)),
            pl.BlockSpec((key_rows, 128), lambda h, i: (0, v_at + h)),
            pl.BlockSpec((8, block), lambda h, i: (h, i)),
            row_spec,
        ],
        out_specs=[row_spec, key_spec, key_spec, pl.BlockSpec((8, 128), lambda h, i: (0, h))],
        out_shape=[
            jax.ShapeDtypeStruct((rows, 128 * pairs), low),
            jax.ShapeDtypeStruct((key_rows, 128 * pairs), low),
            jax.ShapeDtypeStruct((key_rows, 128 * pairs), low),
            jax.ShapeDtypeStruct((8, 128 * pairs), f32),
        ],
        scratch_shapes=[
            pltpu.VMEM((key_rows, 128), f32),
            pltpu.VMEM((key_rows, 128), f32),
            pltpu.VMEM((128, key_rows), low),
        ],
        compiler_params=pltpu.CompilerParams(
            dimension_semantics=("arbitrary", "arbitrary"), vmem_limit_bytes=VMEM_BYTES
        ),
        cost_estimate=pl.CostEstimate(
            flops=40 * rows * key_rows * 512, bytes_accessed=2 * 512 * (4 * rows + 4 * key_rows), transcendentals=0
        ),
    )(queries, keys, values, logs, grad)


def audio_feed(inputs, mixed, weight_out, smalls, ups, weight_up, weight_down, cross_a, cross_b, block):
    rows, width = inputs.shape
    hidden = ups.shape[1]

    def body(step, given, outs, extra):
        inputs, mixed, weight_out, smalls, ups, weight_up, weight_down, cross_a, cross_b = given
        middle_out, norm_out, hidden_out, slope_out, ending_out, memory_out, key_out, value_out = outs
        middle = inputs[...] + dot(mixed[...], weight_out[...]) + row(smalls, 8)
        middle_out[...] = middle
        normed, inverse = norm_rows(middle)
        rounded = (normed * row(smalls, 1) + row(smalls, 4)).astype(low)
        norm_out[...] = rounded
        ending = middle + row(smalls, 9)
        for part in range(hidden // 512):
            cols = slice(part * 512, part * 512 + 512)
            pre = dot(rounded, weight_up[:, cols]) + ups[:, cols].astype(f32)
            value, slope = gelu_both(pre)
            act = value.astype(low)
            hidden_out[:, cols] = act
            slope_out[:, cols] = slope.astype(low)
            ending += dot(act, weight_down[cols, :])
        ending_out[...] = ending
        normed, inverse = norm_rows(ending)
        memory = (normed * row(smalls, 2) + row(smalls, 5)).astype(low)
        memory_out[...] = memory
        key_out[...] = dot(memory, cross_a[...]).astype(low)
        value_out[...] = (dot(memory, cross_b[...]) + row(smalls, 11)).astype(low)

    wide, shape = (rows, hidden), (rows, width)
    return call(
        body, "audio_feed", rows // block, block,
        [(inputs, "rows"), (mixed, "rows"), (weight_out, "side"), (smalls, "full"), (ups, "full"),
         (weight_up, "side"), (weight_down, "side"), (cross_a, "side"), (cross_b, "side")],
        [(shape, f32, "rows"), (shape, low, "rows"), (wide, low, "rows"), (wide, low, "rows"),
         (shape, f32, "rows"), (shape, low, "rows"), (shape, low, "rows"), (shape, low, "rows")],
        flops=2 * rows * width * (3 * width + 2 * hidden),
    )


def text_middle(inputs, mixed, weight_out, smalls, cross_a, block):
    rows, width = inputs.shape

    def body(step, given, outs, extra):
        inputs, mixed, weight_out, smalls, cross_a = given
        middle_out, low_out, query_out = outs
        middle = inputs[...].astype(f32) + dot(mixed[...], weight_out[...]) + row(smalls, 8)
        middle_out[...] = middle
        normed, inverse = norm_rows(middle)
        rounded = (normed * row(smalls, 1) + row(smalls, 4)).astype(low)
        low_out[...] = rounded
        query_out[...] = (dot(rounded, cross_a[...]) + row(smalls, 10)).astype(low) * 0.125

    shape = (rows, width)
    return call(
        body, "text_middle", rows // block, block,
        [(inputs, "rows"), (mixed, "rows"), (weight_out, "side"), (smalls, "full"), (cross_a, "side")],
        [(shape, f32, "rows"), (shape, low, "rows"), (shape, low, "rows")],
        flops=4 * rows * width * width,
    )


def text_feed(length, middle, mixed, cotangent, cross_b, smalls, ups, weight_up, weight_down, block):
    rows, width = middle.shape
    hidden = ups.shape[1]

    def body(step, given, outs, extra):
        length, middle, mixed, cotangent, cross_b, smalls, ups, weight_up, weight_down = given
        decoded_out, norm_out, hidden_out, pre_out, cot_out, grad_out, grad_low, mixed_out, sums, wide_sums = outs
        after = middle[...] + dot(mixed[...], cross_b[...]) + row(smalls, 11)
        normed, inverse = norm_rows(after)
        rounded = (normed * row(smalls, 2) + row(smalls, 5)).astype(low)
        norm_out[...] = rounded
        at_row = lax.broadcasted_iota(jnp.int32, (block, 1), 0) + step * block
        valid = at_row < length[0]
        grad = jnp.where(valid, cotangent[...].astype(f32), 0.0)
        cot = grad.astype(low)
        cot_out[...] = cot
        ending = after + row(smalls, 9)
        back = jnp.zeros((block, width), f32)
        for part in range(hidden // 512):
            cols = slice(part * 512, part * 512 + 512)
            pre = dot(rounded, weight_up[:, cols]) + ups[:, cols].astype(f32)
            value, slope = gelu_both(pre)
            act = value.astype(low)
            hidden_out[:, cols] = act
            ending += dot(act, weight_down[cols, :])
            grad_pre = dot_t(cot, weight_down[cols, :]) * slope
            wide_sums[0:1, cols] += col_sum(grad_pre)
            pre_low = grad_pre.astype(low)
            pre_out[:, cols] = pre_low
            back += dot_t(pre_low, weight_up[:, cols])
        decoded_out[...] = jnp.where(valid, ending, 0.0)
        sums[0:1, :] += col_sum(back * normed)
        sums[1:2, :] += col_sum(back)
        sums[2:3, :] += col_sum(grad)
        grad = grad + norm_back(back, row(smalls, 2), normed, inverse)
        sums[3:4, :] += col_sum(grad)
        grad_out[...] = grad
        rounded = grad.astype(low)
        grad_low[...] = rounded
        mixed_out[...] = dot_t(rounded, cross_b[...]).astype(low)

    wide, shape = (rows, hidden), (rows, width)
    return call(
        body, "text_feed", rows // block, block,
        [(length, "smem"), (middle, "rows"), (mixed, "rows"), (cotangent, "rows"), (cross_b, "side"),
         (smalls, "full"), (ups, "full"), (weight_up, "side"), (weight_down, "side")],
        [(shape, f32, "rows"), (shape, low, "rows"), (wide, low, "rows"), (wide, low, "rows"), (shape, low, "rows"),
         (shape, f32, "rows"), (shape, low, "rows"), (shape, low, "rows"),
         ((8, width), f32, "sums"), ((8, hidden), f32, "sums")],
        flops=2 * rows * width * (2 * width + 4 * hidden),
    )


def text_cross_back(query_grad, middle, grad, smalls, cross_a, weight_out, block):
    rows, width = middle.shape

    def body(step, given, outs, extra):
        query_grad, middle, grad, smalls, cross_a, weight_out = given
        grad_out, low_out, mixed_out, sums = outs
        back = dot_t(query_grad[...], cross_a[...])
        normed, inverse = norm_rows(middle[...])
        sums[0:1, :] += col_sum(back * normed)
        sums[1:2, :] += col_sum(back)
        total = grad[...] + norm_back(back, row(smalls, 1), normed, inverse)
        sums[2:3, :] += col_sum(total)
        grad_out[...] = total
        rounded = total.astype(low)
        low_out[...] = rounded
        mixed_out[...] = dot_t(rounded, weight_out[...]).astype(low)

    shape = (rows, width)
    return call(
        body, "text_cross_back", rows // block, block,
        [(query_grad, "rows"), (middle, "rows"), (grad, "rows"), (smalls, "full"), (cross_a, "side"), (weight_out, "side")],
        [(shape, f32, "rows"), (shape, low, "rows"), (shape, low, "rows"), ((8, width), f32, "sums")],
        flops=4 * rows * width * width,
    )


def project_back(query_grad, key_grad, value_grad, inputs, grad, smalls, weight, block):
    rows, width = inputs.shape

    def body(step, given, outs, extra):
        query_grad, key_grad, value_grad, inputs, grad, smalls, weight = given
        grad_out, sums = outs
        back = (
            dot_t(query_grad[...], weight[:, :width])
            + dot_t(key_grad[...], weight[:, width : 2 * width])
            + dot_t(value_grad[...], weight[:, 2 * width :])
        )
        normed, inverse = norm_rows(inputs[...].astype(f32))
        sums[0:1, :] += col_sum(back * normed)
        sums[1:2, :] += col_sum(back)
        grad_out[...] = grad[...] + norm_back(back, row(smalls, 0), normed, inverse)

    return call(
        body, "project_back", rows // block, block,
        [(query_grad, "rows"), (key_grad, "rows"), (value_grad, "rows"), (inputs, "rows"), (grad, "rows"),
         (smalls, "full"), (weight, "side")],
        [((rows, width), f32, "rows"), ((8, width), f32, "sums")],
        flops=6 * rows * width * width,
    )


def audio_feed_back(key_grad, value_grad, ending, middle, slope, smalls, cross_a, cross_b, weight_up, weight_down, weight_out, block):
    rows, width = ending.shape
    hidden = slope.shape[1]

    def body(step, given, outs, extra):
        key_grad, value_grad, ending, middle, slope, smalls, cross_a, cross_b, weight_up, weight_down, weight_out = given
        end_low, pre_out, grad_out, grad_low, mixed_out, sums, wide_sums = outs
        back = dot_t(key_grad[...], cross_a[...]) + dot_t(value_grad[...], cross_b[...])
        normed, inverse = norm_rows(ending[...])
        sums[0:1, :] += col_sum(back * normed)
        sums[1:2, :] += col_sum(back)
        grad = norm_back(back, row(smalls, 2), normed, inverse)
        sums[2:3, :] += col_sum(grad)
        rounded = grad.astype(low)
        end_low[...] = rounded
        back = jnp.zeros((block, width), f32)
        for part in range(hidden // 512):
            cols = slice(part * 512, part * 512 + 512)
            grad_pre = dot_t(rounded, weight_down[cols, :]) * slope[:, cols].astype(f32)
            wide_sums[0:1, cols] += col_sum(grad_pre)
            pre_low = grad_pre.astype(low)
            pre_out[:, cols] = pre_low
            back += dot_t(pre_low, weight_up[:, cols])
        normed, inverse = norm_rows(middle[...])
        sums[3:4, :] += col_sum(back * normed)
        sums[4:5, :] += col_sum(back)
        grad = grad + norm_back(back, row(smalls, 1), normed, inverse)
        sums[5:6, :] += col_sum(grad)
        grad_out[...] = grad
        rounded = grad.astype(low)
        grad_low[...] = rounded
        mixed_out[...] = dot_t(rounded, weight_out[...]).astype(low)

    wide, shape = (rows, hidden), (rows, width)
    return call(
        body, "audio_feed_back", rows // block, block,
        [(key_grad, "rows"), (value_grad, "rows"), (ending, "rows"), (middle, "rows"), (slope, "rows"), (smalls, "full"),
         (cross_a, "side"), (cross_b, "side"), (weight_up, "side"), (weight_down, "side"), (weight_out, "side")],
        [(shape, low, "rows"), (wide, low, "rows"), (shape, f32, "rows"), (shape, low, "rows"), (shape, low, "rows"),
         ((8, width), f32, "sums"), ((8, hidden), f32, "sums")],
        flops=2 * rows * width * (3 * width + 2 * hidden),
    )


def stem_back(query_grad, key_grad, value_grad, encoded, grad, smalls, weight, slope_second, second, even_slope, odd_slope, first, block):
    rows, width = encoded.shape

    def body(step, given, outs, extra):
        query_grad, key_grad, value_grad, encoded, grad, smalls, weight, slope_second, second, even_slope, odd_slope, first = given
        second_low, next_low, even_low, odd_low, taps_out, sums = outs
        (carry,) = extra

        @pl.when(step == 0)
        def _():
            carry[...] = jnp.zeros(carry.shape, f32)

        back = (
            dot_t(query_grad[...], weight[:, :width])
            + dot_t(key_grad[...], weight[:, width : 2 * width])
            + dot_t(value_grad[...], weight[:, 2 * width :])
        )
        normed, inverse = norm_rows(encoded[...])
        sums[0:1, :] += col_sum(back * normed)
        sums[1:2, :] += col_sum(back)
        total = grad[...] + norm_back(back, row(smalls, 0), normed, inverse)
        total = total * slope_second[...].astype(f32)
        sums[2:3, :] += col_sum(total)
        rounded = total.astype(low)
        second_low[...] = rounded
        at_row = lax.broadcasted_iota(jnp.int32, (block, width), 0)
        wide = rounded.astype(f32)
        moved = jnp.where(at_row == block - 1, carry[0:1, :], pltpu.roll(wide, block - 1, 0))
        carry[0:1, :] = wide[0:1, :]
        moved = moved.astype(low)
        next_low[...] = moved
        moved = dot_t(moved, second[0])
        grad_even = dot_t(rounded, second[1]) * even_slope[...].astype(f32)
        grad_odd = (dot_t(rounded, second[2]) + moved) * odd_slope[...].astype(f32)
        sums[3:4, :] += col_sum(grad_even) + col_sum(grad_odd)
        grad_even = grad_even.astype(low)
        grad_odd = grad_odd.astype(low)
        even_low[...] = grad_even
        odd_low[...] = grad_odd
        taps_even = dot_t(grad_even, first[...])
        taps_odd = dot_t(grad_odd, first[...])
        taps_out[:, 0:128] = taps_even[:, 0:128]
        taps_out[:, 128:256] = taps_even[:, 128:256] + taps_odd[:, 0:128]
        taps_out[:, 256:384] = taps_even[:, 256:384] + taps_odd[:, 128:256]
        taps_out[:, 384:512] = taps_odd[:, 256:384]

    shape = (rows, width)
    return call(
        body, "stem_back", rows // block, block,
        [(query_grad, "rows"), (key_grad, "rows"), (value_grad, "rows"), (encoded, "rows"), (grad, "rows"), (smalls, "full"),
         (weight, "side"), (slope_second, "rows"), (second, "full"), (even_slope, "rows"), (odd_slope, "rows"), (first, "full")],
        [(shape, low, "rows")] * 4 + [((rows, 512), f32, "rows"), ((8, width), f32, "sums")],
        scratch=[pltpu.VMEM((8, width), f32)],
        reverse=True,
        flops=2 * rows * width * (6 * width + 768),
    )


def weight_grads(audio, text, taps, even_low, odd_low, conv, small, flat_rows):
    width = 512
    frames, text_rows = taps.shape[0], text[0][0].shape[0]
    jobs_audio = audio + conv
    arrays, places = [], {}

    def place(array):
        if id(array) not in places:
            places[id(array)] = len(arrays)
            arrays.append(array)
        return places[id(array)]

    lists = [
        [(place(x), xc, place(y), yc) for x, xc, y, yc in jobs] for jobs in (jobs_audio, text)
    ]
    at_taps, at_even, at_odd, at_small = place(taps), place(even_low), place(odd_low), place(small)
    base = len(audio) * width
    half = width // 2
    first_base, small_base = base + 3 * half, base + 3 * half + 192

    def kernel(*refs):
        given, flat = refs[: len(arrays)], refs[len(arrays)]
        x_audio, y_audio, x_text, y_text, out_buf, first_buf, in_sem, out_sem, first_sem, small_sem = refs[len(arrays) + 1 :]

        def small_copies():
            here = pl.ds(small_base, small.shape[1])
            return [pltpu.make_async_copy(given[at_small].at[s], flat.at[s, here], small_sem.at[s]) for s in range(2)]

        for copy in small_copies():
            copy.start()

        def run(side, jobs, x_buf, y_buf, plain):
            count = len(jobs)

            def copies(job, slot):
                x, xc, y, yc = job
                return (
                    pltpu.make_async_copy(given[x].at[:, xc * width : (xc + 1) * width], x_buf.at[slot], in_sem.at[0, slot]),
                    pltpu.make_async_copy(given[y].at[:, yc * width : (yc + 1) * width], y_buf.at[slot], in_sem.at[1, slot]),
                )

            def fetch(i, slot):
                for n, job in enumerate(jobs):

                    @pl.when(i == n)
                    def _(job=job):
                        for copy in copies(job, slot):
                            copy.start()

            def out_wait(slot):
                pltpu.make_async_copy(out_buf.at[slot], flat.at[0, 0:width], out_sem.at[slot]).wait()

            fetch(0, 0)

            @pl.loop(0, count)
            def _(i):
                slot = i % 2

                @pl.when(i + 1 < count)
                def _():
                    fetch(i + 1, 1 - slot)

                for copy in copies(jobs[0], slot):
                    copy.wait()

                @pl.when(i >= 2)
                def _():
                    out_wait(slot)

                out_buf[slot] = dot_tt(x_buf[slot], y_buf[slot]).astype(low)

                @pl.when(i < plain)
                def _():
                    pltpu.make_async_copy(
                        out_buf.at[slot], flat.at[side, pl.ds(pl.multiple_of(i * width, width), width)], out_sem.at[slot]
                    ).start()

                for tap in range(count - plain):

                    @pl.when(i == plain + tap)
                    def _(tap=tap):
                        for s in range(2):
                            cols = slice(s * half, s * half + half)
                            start = tap * width
                            for block in range(2):
                                r = start + block * half
                                left = r < 3 * half
                                to = base + (r if left else r - 3 * half)
                                pltpu.make_async_copy(
                                    out_buf.at[slot, block * half : block * half + half, cols],
                                    flat.at[s, to : to + half, 0:half] if left else flat.at[s, to : to + half, half:width],
                                    out_sem.at[slot],
                                ).start()

            for i in range(count - 2, count):
                out_wait(i % 2)

        run(0, lists[0], x_audio, y_audio, len(audio))
        run(1, lists[1], x_text, y_text, len(text))

        copies = [
            pltpu.make_async_copy(given[at_taps].at[:, 0:384], x_audio.at[0, :, 0:384], in_sem.at[0, 0]),
            pltpu.make_async_copy(given[at_even], y_audio.at[0], in_sem.at[1, 0]),
            pltpu.make_async_copy(given[at_taps].at[:, 128:512], x_audio.at[1, :, 0:384], in_sem.at[0, 1]),
            pltpu.make_async_copy(given[at_odd], y_audio.at[1], in_sem.at[1, 1]),
        ]
        for copy in copies:
            copy.start()
        for copy in copies:
            copy.wait()
        total = dot_tt(x_audio[0, :, 0:384], y_audio[0]) + dot_tt(x_audio[1, :, 0:384], y_audio[1])
        first_buf[...] = total.astype(low)
        copies = [
            pltpu.make_async_copy(
                first_buf.at[b * 192 : b * 192 + 192, s * half : s * half + half],
                flat.at[s, first_base : first_base + 192, b * half : b * half + half],
                first_sem.at[s, b],
            )
            for s in range(2)
            for b in range(2)
        ]
        for copy in copies:
            copy.start()
        for copy in copies + small_copies():
            copy.wait()

    return pl.pallas_call(
        kernel,
        name="weight_grads",
        in_specs=[pl.BlockSpec(memory_space=pl.ANY)] * len(arrays),
        out_specs=pl.BlockSpec(memory_space=pl.ANY),
        out_shape=jax.ShapeDtypeStruct((2, flat_rows, width), low),
        scratch_shapes=[
            pltpu.VMEM((2, frames, width), low),
            pltpu.VMEM((2, frames, width), low),
            pltpu.VMEM((2, text_rows, width), low),
            pltpu.VMEM((2, text_rows, width), low),
            pltpu.VMEM((2, width, width), low),
            pltpu.VMEM((384, width), low),
            pltpu.SemaphoreType.DMA((2, 2)),
            pltpu.SemaphoreType.DMA((2,)),
            pltpu.SemaphoreType.DMA((2, 2)),
            pltpu.SemaphoreType.DMA((2,)),
        ],
        compiler_params=pltpu.CompilerParams(vmem_limit_bytes=VMEM_BYTES),
        cost_estimate=pl.CostEstimate(
            flops=2 * width * width * (frames * (len(jobs_audio) + 2) + text_rows * len(text)),
            bytes_accessed=sum(2 * a.size for a in arrays), transcendentals=0,
        ),
    )(*arrays)


def factors_of(size):
    found, rest = [], size // 2
    while rest > 1:
        radix = 2 if rest in (2, 8) or rest % 4 else 4
        found.append(radix)
        rest //= radix
    return found


def reduce_all(flat):
    rows, width = flat.shape[1:]
    replicas = lax.axis_size("dp")
    factors = factors_of(replicas)
    chunk = max(512, 16 * replicas)
    count = rows // chunk
    half = chunk // 2
    sizes = []
    for radix in factors:
        sizes.append((sizes[-1] if sizes else half) // radix)
    levels = len(factors)

    def kernel(flat_ref, out_ref, acc, core_recv, side_recv, work, final, *refs):
        recvs = refs[:levels]
        local_sem, out_sem, core_sem, side_sem, back_sem = refs[levels : levels + 5]
        rs_sems = refs[levels + 5 : 2 * levels + 5]
        ag_sems = refs[2 * levels + 5 :]
        section, replica = lax.axis_index("section"), lax.axis_index("dp")
        core = replica % 2
        digits, strides, rest, stride = [], [], replica // 2, 2
        for radix in factors:
            digits.append(rest % radix)
            strides.append(stride)
            rest, stride = rest // radix, stride * radix
        core_peer = {"dp": replica + 1 - 2 * core}
        side_peer = {"section": 1 - section}

        def peer(level, distance):
            digit = (digits[level] + distance) % factors[level]
            return digit, {"dp": replica + (digit - digits[level]) * strides[level]}

        def remote(source, target, sems, at, device):
            return pltpu.make_async_remote_copy(
                src_ref=source, dst_ref=target, send_sem=sems.at[(0,) + at], recv_sem=sems.at[(1,) + at],
                device_id=device, device_id_type=pl.DeviceIdType.MESH,
            )

        def start_of(k, level):
            row_at = k * chunk + core * half
            for n in range(level):
                row_at = row_at + digits[n] * sizes[n]
            return row_at

        def place_of(k, level):
            return start_of(k, level) - k * chunk - core * half + k * half

        def rows_at(start, size):
            return pl.ds(pl.multiple_of(start, 16), size)

        def load(k):
            return pltpu.make_async_copy(
                flat_ref.at[:, rows_at(k * chunk + core * half, half)], acc.at[:, rows_at(k * half, half)], local_sem.at[k]
            )

        def core_copy(k):
            return remote(
                flat_ref.at[:, rows_at(k * chunk + (1 - core) * half, half)],
                core_recv.at[:, rows_at(k * half, half)], core_sem, (k,), core_peer,
            )

        def side_copy(k):
            return remote(acc.at[1 - section, rows_at(k * half, half)], side_recv.at[rows_at(k * half, half)], side_sem, (k,), side_peer)

        def scatter_copy(k, level, distance):
            digit, device = peer(level, distance)
            size = sizes[level]
            return remote(
                work.at[rows_at(place_of(k, level) + digit * size, size)],
                recvs[level].at[distance - 1, rows_at(k * size, size)], rs_sems[level], (distance - 1, k), device,
            )

        def gather_copy(k, level, distance):
            digit, device = peer(level, distance)
            here = final.at[rows_at(start_of(k, level + 1), sizes[level])]
            return remote(here, here, ag_sems[level], (distance - 1, k), device)

        def back_copy(k):
            here = final.at[rows_at(k * chunk + core * half, half)]
            return remote(here, here, back_sem, (k,), core_peer)

        def store(k):
            here = rows_at(k * chunk, chunk)
            return pltpu.make_async_copy(final.at[here], out_ref.at[here], out_sem.at[k])

        def stage_core(k):
            load(k).wait()
            core_copy(k).wait_recv()
            here = rows_at(k * half, half)
            acc[:, here] = (acc[:, here].astype(f32) + core_recv[:, here].astype(f32)).astype(low)
            side_copy(k).start()

        def stage_side(k):
            side_copy(k).wait_recv()
            here = rows_at(k * half, half)
            work[here] = (
                acc[section, here].astype(f32) + side_recv[here].astype(f32)
            ).astype(low)
            for distance in range(1, factors[0]):
                scatter_copy(k, 0, distance).start()

        def stage_scatter(k, level):
            size = sizes[level]
            for distance in range(1, factors[level]):
                scatter_copy(k, level, distance).wait_recv()
            here = rows_at(place_of(k, level + 1), size)
            total = work[here].astype(f32)
            for distance in range(1, factors[level]):
                total += recvs[level][distance - 1, rows_at(k * size, size)].astype(f32)
            if level + 1 < levels:
                work[here] = total.astype(low)
                for distance in range(1, factors[level + 1]):
                    scatter_copy(k, level + 1, distance).start()
            else:
                final[rows_at(start_of(k, level + 1), size)] = total.astype(low)
                for distance in range(1, factors[level]):
                    gather_copy(k, level, distance).start()

        def stage_gather(k, level):
            for distance in range(1, factors[level]):
                gather_copy(k, level, distance).wait_recv()
            if level > 0:
                for distance in range(1, factors[level - 1]):
                    gather_copy(k, level - 1, distance).start()
            else:
                back_copy(k).start()

        def stage_back(k):
            back_copy(k).wait_recv()
            store(k).start()

        stages = [stage_core, stage_side]
        stages += [functools.partial(stage_scatter, level=n) for n in range(levels)]
        stages += [functools.partial(stage_gather, level=n) for n in reversed(range(levels))]
        stages.append(stage_back)

        barrier = pltpu.get_barrier_semaphore()
        peers = [core_peer, side_peer]
        peers += [peer(n, d)[1] for n in range(levels) for d in range(1, factors[n])]
        for device in peers:
            pl.semaphore_signal(barrier, inc=1, device_id=device, device_id_type=pl.DeviceIdType.MESH)
        pl.semaphore_wait(barrier, len(peers))

        @pl.loop(0, count)
        def _(k):
            load(k).start()
            core_copy(k).start()

        @pl.loop(0, count + len(stages) - 1)
        def _(tick):
            for n, stage in enumerate(stages):

                @pl.when(jnp.logical_and(tick >= n, tick < count + n))
                def _(n=n, stage=stage):
                    stage(tick - n)

        @pl.loop(0, count)
        def _(k):
            core_copy(k).wait_send()
            side_copy(k).wait_send()
            for level in range(levels):
                for distance in range(1, factors[level]):
                    scatter_copy(k, level, distance).wait_send()
                    gather_copy(k, level, distance).wait_send()
            back_copy(k).wait_send()
            store(k).wait()

    def sems(*shape):
        return pltpu.SemaphoreType.DMA(shape)

    return pl.pallas_call(
        kernel,
        name="reduce_all",
        in_specs=[pl.BlockSpec(memory_space=pl.ANY)],
        out_specs=pl.BlockSpec(memory_space=pl.ANY),
        out_shape=jax.ShapeDtypeStruct((rows, width), low),
        scratch_shapes=[
            pltpu.VMEM((2, rows // 2, width), low),
            pltpu.VMEM((2, rows // 2, width), low),
            pltpu.VMEM((rows // 2, width), low),
            pltpu.VMEM((rows // 2, width), low),
            pltpu.VMEM((rows, width), low),
            *[pltpu.VMEM((r - 1, count * s, width), low) for r, s in zip(factors, sizes)],
            sems(count), sems(count), sems(2, count), sems(2, count), sems(2, count),
            *[sems(2, r - 1, count) for r in factors],
            *[sems(2, r - 1, count) for r in factors],
        ],
        compiler_params=pltpu.CompilerParams(
            collective_id=0, has_side_effects=True, vmem_limit_bytes=VMEM_BYTES
        ),
        cost_estimate=pl.CostEstimate(flops=0, bytes_accessed=100 * flat.size, transcendentals=0),
    )(flat)


def shards(
    mel_input,
    time_start,
    time_width,
    freq_start,
    freq_width,
    text_len,
    text_embed,
    cotangent,
    positions,
    conv_first,
    conv_first_bias,
    conv_second,
    norm_gain,
    norm_shift,
    attn_in,
    attn_out,
    mlp_up,
    mlp_down,
    up_bias,
    small_bias,
    cross_first,
    cross_second,
):
    mine = lax.axis_index("section")
    is_first = mine == 0
    frames, width = positions.shape
    bands, mel_frames = mel_input.shape[1], mel_input.shape[2]
    text_rows = text_embed.shape[1]
    audio_block = 256
    text_block = 224
    swap_pairs = [(0, 1), (1, 0)]

    def own(array):
        return lax.dynamic_index_in_dim(array, mine, 0, keepdims=False)

    def partner(array):
        return lax.ppermute(array, "section", swap_pairs)

    packed = jnp.concatenate(
        [norm_gain[0], norm_shift[0], small_bias[0], up_bias[0].reshape(-1, width)], axis=0
    )
    conv_own = jnp.concatenate([conv_first.reshape(-1, width // 2), conv_first_bias[None]], axis=0)
    conv_other = partner(conv_own)
    second_other = partner(conv_second)
    packed_other = partner(packed)
    others = [partner(w) for w in (attn_in, attn_out, mlp_up, mlp_down, cross_first, cross_second)]
    owns = (attn_in, attn_out, mlp_up, mlp_down, cross_first, cross_second)
    a_in, a_out, a_up, a_down, a_cross_a, a_cross_b = [Side(0, o, p) for o, p in zip(owns, others)]
    t_in, t_out, t_up, t_down, t_cross_a, t_cross_b = [Side(1, o, p) for o, p in zip(owns, others)]

    def ordered(first, second):
        return jnp.where(
            is_first,
            jnp.concatenate([first, second], axis=-1),
            jnp.concatenate([second, first], axis=-1),
        )

    conv_all = ordered(conv_own, conv_other)
    second_all = ordered(conv_second, second_other)
    first_all = jnp.pad(
        conv_all[: 3 * bands].reshape(3, bands, width), ((0, 0), (0, 128 - bands), (0, 0))
    ).reshape(384, width)
    first_bias = conv_all[3 * bands :].astype(f32)
    a_packed = jnp.where(is_first, packed, packed_other).astype(f32)
    t_packed = jnp.where(is_first, packed_other, packed).astype(f32)
    a_small, a_ups = a_packed[:12], a_packed[12:].reshape(1, -1)
    t_small, t_ups = t_packed[:12], t_packed[12:].reshape(1, -1)

    frame_at = jnp.arange(mel_frames, dtype=jnp.int32)
    band_at = jnp.arange(bands, dtype=jnp.int32)
    begin, band = own(time_start), own(freq_start)
    keep = jnp.logical_and(
        jnp.logical_or(band_at < band, band_at >= band + own(freq_width))[:, None],
        jnp.logical_or(frame_at < begin, frame_at >= begin + own(time_width))[None, :],
    )
    mel_clip = own(mel_input)
    masked = jnp.where(keep, mel_clip, jnp.zeros_like(mel_clip)).T.reshape(frames, 2, bands)
    masked = jnp.pad(masked, ((0, 0), (0, 0), (0, 128 - bands)))
    even, odd = masked[:, 0], masked[:, 1]
    taps = jnp.concatenate(
        [jnp.pad(odd, ((1, 0), (0, 0)))[:-1], even, odd, jnp.pad(even, ((0, 1), (0, 0)))[1:]], axis=1
    )

    encoded, even_act, odd_act, even_slope, odd_slope, slope_second = stem(
        taps, first_all, first_bias, second_all, a_small, positions
    )
    a_norm, a_joint = project(encoded, a_in, a_small, audio_block)
    a_mixed, a_logs = attend(a_joint, a_joint, a_joint, (0, 4, 8), False, audio_block)
    a_middle, a_feed_norm, a_hidden, a_slope, a_ending, memory, memory_keys, memory_values = audio_feed(
        encoded, a_mixed, a_out, a_small, a_ups, a_up, a_down, a_cross_a, a_cross_b, audio_block
    )

    text_clip, cot_clip = own(text_embed), own(cotangent)
    t_norm, t_joint = project(text_clip, t_in, t_small, text_block)
    t_mixed, t_logs = attend(t_joint, t_joint, t_joint, (0, 4, 8), True, text_rows)
    t_middle, cross_low, cross_query = text_middle(text_clip, t_mixed, t_out, t_small, t_cross_a, text_block)
    c_mixed, c_logs = attend(cross_query, memory_keys, memory_values, (0, 0, 0), False, text_rows)
    (
        decoded, t_feed_norm, t_hidden, t_pre, cot_low, after_grad, after_low, c_mixed_grad, feed_sums, feed_wide,
    ) = text_feed(
        own(text_len)[None], t_middle, c_mixed, cot_clip, t_cross_b, t_small, t_ups, t_up, t_down, text_block
    )
    query_grad, key_grad, value_grad, c_sums = attend_back(
        cross_query, memory_keys, memory_values, (0, 0, 0), c_logs, c_mixed_grad, False, True, text_rows
    )
    middle_grad, middle_low, t_mixed_grad, cross_sums = text_cross_back(
        query_grad, t_middle, after_grad, t_small, t_cross_a, t_out, text_block
    )
    tq_grad, tk_grad, tv_grad, t_sums = attend_back(
        t_joint, t_joint, t_joint, (0, 4, 8), t_logs, t_mixed_grad, True, False, text_rows
    )
    text_grad, text_sums = project_back(
        tq_grad, tk_grad, tv_grad, text_clip, middle_grad, t_small, t_in, text_block
    )

    end_low, a_pre, a_grad, a_grad_low, a_mixed_grad, a_feed_sums, a_feed_wide = audio_feed_back(
        key_grad, value_grad, a_ending, a_middle, a_slope, a_small, a_cross_a, a_cross_b, a_up, a_down, a_out, audio_block
    )
    aq_grad, ak_grad, av_grad, a_sums = attend_back(
        a_joint, a_joint, a_joint, (0, 4, 8), a_logs, a_mixed_grad, False, False, audio_block
    )
    second_low, next_low, even_low, odd_low, taps_grad, stem_sums = stem_back(
        aq_grad, ak_grad, av_grad, encoded, a_grad, a_small, a_in, slope_second, second_all,
        even_slope, odd_slope, first_all, audio_block,
    )
    odd_grad = taps_grad[:, 256 : 256 + bands] + jnp.pad(taps_grad[1:, 0:bands], ((0, 1), (0, 0)))
    even_grad = taps_grad[:, 128 : 128 + bands] + jnp.pad(taps_grad[:-1, 384 : 384 + bands], ((1, 0), (0, 0)))
    mel_grad = jnp.stack([even_grad, odd_grad], axis=1).reshape(mel_frames, bands).T
    mel_grad = jnp.where(keep, mel_grad, 0.0)

    half = width // 2

    a_rows = jnp.stack(
        [
            stem_sums[0], a_feed_sums[3], a_feed_sums[0], stem_sums[1], a_feed_sums[4], a_feed_sums[1],
            a_sums[0], a_sums[1], a_feed_sums[5], a_feed_sums[2], stem_sums[2], c_sums[1],
        ]
    )
    t_rows = jnp.stack(
        [
            text_sums[0], cross_sums[0], feed_sums[0], text_sums[1], cross_sums[1], feed_sums[1],
            t_sums[0], t_sums[1], cross_sums[2], feed_sums[2], c_sums[0], feed_sums[3],
        ]
    )
    bias_row = jnp.pad(stem_sums[3].reshape(2, 1, half), ((0, 0), (0, 0), (0, half)))
    wide_rows = jnp.stack([a_feed_wide[0].reshape(-1, width), feed_wide[0].reshape(-1, width)])
    small = jnp.concatenate([jnp.stack([a_rows, t_rows]), wide_rows, bias_row], axis=1).astype(low)
    small = jnp.pad(small, ((0, 0), (0, 32 - small.shape[1]), (0, 0)))
    audio = [(a_norm, 0, part, 0) for part in (aq_grad, ak_grad, av_grad)] + [(a_mixed, 0, a_grad_low, 0)]
    audio += [(a_feed_norm, 0, a_pre, n) for n in range(4)] + [(a_hidden, n, end_low, 0) for n in range(4)]
    audio += [(memory, 0, key_grad, 0), (memory, 0, value_grad, 0)]
    text = [(t_norm, 0, part, 0) for part in (tq_grad, tk_grad, tv_grad)] + [(t_mixed, 0, middle_low, 0)]
    text += [(t_feed_norm, 0, t_pre, n) for n in range(4)] + [(t_hidden, n, cot_low, 0) for n in range(4)]
    text += [(cross_low, 0, query_grad, 0), (c_mixed, 0, after_low, 0)]
    conv = [(odd_act, 0, next_low, 0), (even_act, 0, second_low, 0), (odd_act, 0, second_low, 0)]
    flat = weight_grads(audio, text, taps, even_low, odd_low, conv, small, 16 * 512)
    total = reduce_all(flat).astype(f32)

    def tiles(first, count):
        return [total[n * 512 : n * 512 + 512] for n in range(first, first + count)]

    def unfold(start, count):
        part = total[start : start + count]
        return jnp.concatenate([part[:, :half], part[:, half:]], axis=0)

    conv_at = 14 * 512
    small_at = conv_at + 768 + 192
    rows_out = total[small_at : small_at + 12]
    first_grad = unfold(conv_at + 768, 192).reshape(3, 128, half)[:, :bands]

    def swap(array, axis):
        size = array.shape[axis] // 2
        first = lax.slice_in_dim(array, 0, size, axis=axis)
        second = lax.slice_in_dim(array, size, 2 * size, axis=axis)
        keep_part = jnp.where(is_first, first, second)
        got = partner(jnp.where(is_first, second, first).astype(low)).astype(f32)
        return jnp.where(is_first, jnp.stack([keep_part, got]), jnp.stack([got, keep_part]))

    cross_row = lax.ppermute(rows_out[11].astype(low), "section", [(1, 0)]).astype(f32)
    cross_bias = jnp.where(is_first, cross_row[:half], rows_out[11][half:])
    return (
        swap(decoded, 1),
        swap(text_grad, 1),
        swap(mel_grad, 1),
        first_grad,
        total[small_at + 16, :half],
        unfold(conv_at, 768).reshape(3, 512, half),
        rows_out[None, 0:3],
        rows_out[None, 3:6],
        jnp.concatenate(tiles(0, 3), axis=1)[None],
        total[None, 1536:2048],
        jnp.concatenate(tiles(4, 4), axis=1)[None],
        total[None, 4096:6144],
        total[small_at + 12 : small_at + 16].reshape(1, -1),
        rows_out[None, 6:12],
        total[None, 6144:6656],
        total[None, 6656:7168],
        cross_bias,
    )


def solution(mesh):
    return jax.shard_map(
        shards,
        mesh=mesh,
        in_specs=(
            P("dp", None, None),
            P("dp"),
            P("dp"),
            P("dp"),
            P("dp"),
            P("dp"),
            P("dp", None, None),
            P("dp", None, None),
            P(),
            P(None, None, "section"),
            P("section"),
            P(None, None, "section"),
            P("section", None, None),
            P("section", None, None),
            P("section", None, None),
            P("section", None, None),
            P("section", None, None),
            P("section", None, None),
            P("section", None),
            P("section", None, None),
            P("section", None, None),
            P("section", None, None),
        ),
        out_specs=(
            P("dp", None, "section"),
            P("dp", None, "section"),
            P("dp", None, "section"),
            P(None, None, "section"),
            P("section"),
            P(None, None, "section"),
            P("section", None, None),
            P("section", None, None),
            P("section", None, None),
            P("section", None, None),
            P("section", None, None),
            P("section", None, None),
            P("section", None),
            P("section", None, None),
            P("section", None, None),
            P("section", None, None),
            P("section"),
        ),
        check_vma=False,
    )
```

time: 1050 us -> 586 us (0.56)
  Pallas kernels: 0 us -> 359 us
  waiting for transfers between devices: 419 us -> 118 us
  matrix products: 247 us -> 0 us
  local copies, waits for them, and re-layouts: 149 us -> 42.7 us
  blocking collectives: 94.8 us -> 0 us
  other arithmetic: 105 us -> 39.8 us
  between operations: 19.8 us -> 4.33 us
  starting transfers between devices: 4.46 us -> 16.6 us
    pallas_call x0 -> x18, Pallas kernels: none -> 359 us  [the longest x1 124 us: reduce_all(): pl.pallas_call(kernel, name='reduce_all', in_specs=[pl.BlockSpec(memory_s...]
    dot_general x80 -> x0, matrix products: 247 us -> none  [the longest x4 39.9 us: one_block(): jnp.einsum('qhd,khd->hqk', grad_block, value_heads, preferred_element_typ...]
    reduce_scatter x1 -> x0, waiting for transfers between devices: 182 us -> none  [shards(): lax.psum_scatter(flat, 'section', scatter_dimension=0, tiled=False)]
    ppermute x4 -> x13, waiting for transfers between devices: 1.18 us -> 118 us  [the longest x12 112 us: partner(): return lax.ppermute(array, 'section', swap_pairs)]
    all_gather x7 -> x0, waiting for transfers between devices: 115 us -> none  [the longest x6 115 us: both(): return lax.all_gather(weight, 'section', axis=0, tiled=False)]
    psum x1 -> x0, waiting for transfers between devices: 101 us -> none  [shards(): flat_all = lax.psum(flat_shard, 'dp').astype(jnp.float32)]
    psum x1 -> x0, blocking collectives: 64.1 us -> none  [shards(): lax.psum(lax.psum_scatter(small_flat, 'section', scatter_dimension=0, til...]
    reduce_sum x21 -> x0, other arithmetic: 37.4 us -> none  [the longest x4 11.3 us: one_block(): row_total = jnp.sum(exponent, axis=-1, keepdims=True)]
  transfers between devices with their start and end apart: 14 -> 13, of which waited for: 8 -> 5; matrix products, arithmetic and copies ran while one was open for 12% -> 6% of each run, Pallas kernels for 0% -> 9%
where the time goes in v2:
time: 586 us; the launch traced here: 581 us
  Pallas kernels  359 us (61%)
  waiting for transfers between devices  118 us (20%)
  local copies, waits for them, and re-layouts  42.7 us (7%)
  other arithmetic  39.8 us (7%)
  starting transfers between devices  16.6 us (3%)
    pallas_call x1, Pallas kernels, reduce_all(): pl.pallas_call(kernel, name='reduce_all', in_specs=[pl.BlockSpec(memory_s...  124 us
    ppermute x12, waiting for transfers between devices, partner(): return lax.ppermute(array, 'section', swap_pairs)  112 us
    pallas_call x10, Pallas kernels, call(): pl.pallas_call(kernel, name=name, grid=(steps,), in_specs=specs, out_spec...  101 us
    pallas_call x3, Pallas kernels, attend_back(): pl.pallas_call(kernel, name='attend_back', grid=(pairs, steps), in_specs=...  56.6 us
    pallas_call x1, Pallas kernels, weight_grads(): pl.pallas_call(kernel, name='weight_grads', in_specs=[pl.BlockSpec(memory...  41.9 us
    pallas_call x3, Pallas kernels, attend(): pl.pallas_call(kernel, name='attend', grid=(pairs, steps), in_specs=[pl.B...  36.4 us
    ppermute x12, starting transfers between devices, partner(): return lax.ppermute(array, 'section', swap_pairs)  15.4 us
  transfers between devices with their start and end apart: 13, of which 5 were waited for; matrix products, arithmetic and copies ran while one was open for 6% of the time, Pallas kernels for 9%

profile of v2, /device:TPU:0, one launch (start us, length us, event | category | flops | bytes accessed | tf_op | source)
XLA Modules:
  0.0 580.6 jit_solution(1677215118318388139)
XLA Ops:
  0.7 3.0 collective-permute-start
  6.0 1.6 pad_maximum_fusion.4
  7.5 1.9 collective-permute-start.4
  9.6 1.9 collective-permute-start.6
  11.5 1.0 constant_dynamic-slice_fusion
  12.8 1.2 dynamic_slice.29
  14.0 1.2 dynamic_slice.30
  17.2 1.2 dynamic_slice.31
  18.5 1.2 dynamic_slice.32
  22.3 0.8 dynamic-slice_bitcast_fusion.1.refs_0_.refs_3_
  23.3 1.1 pad_maximum_fusion.1.refs_0_.refs_31_
  25.8 13.7 %collective-permute-done.1 = bf16[16,512]{1,0:T(8,128)(2,1)S(1)} collective-permute-done((bf16[16,512]{1,0:T(8,128)(2,1)S(1)}, bf16[16,512]{1,0:T(8,128)(2,1)S(1)}, u32[]{:S(2)}, u32[]{:S(2)}) %collective-permute-start.1) | collective-permute-done | bytes 16416 | tf_op jit(solution)/shard_map/ppermute | solution.py:1027
  39.5 2.1 collective-permute-start.7
  42.8 1.4 collective-permute-start.2
  45.8 13.4 %collective-permute-done.5 = bf16[3,512,256]{2,1,0:T(8,128)(2,1)} collective-permute-done((bf16[3,512,256]{2,1,0:T(8,128)(2,1)}, bf16[3,512,256]{2,1,0:T(8,128)(2,1)}, u32[]{:S(2)}, u32[]{:S(2)}) %collective-permute-start.5) | collective-permute-done | bytes 786464 | tf_op jit(solution)/shard_map/ppermute | solution.py:1027
  59.2 2.1 collective-permute-start.3
  61.2 3.5 maximum_select_fusion.refs_3_.refs_9_
  64.7 10.6 %stem.1 = (f32[1024,512]{1,0:T(8,128)}, bf16[1024,512]{1,0:T(8,128)(2,1)}, bf16[1024,512]{1,0:T(8,128)(2,1)}, bf16[1024,512]{1,0:T(8,128)(2,1)}, bf16[1024,512]{1,0:T(8,128)(2,1)}, /*index=5*/bf16[1024,512]{1,0:T(8,128)(2,1)}) custom-call(bf16[1024,512]{1,0:T(8,128)(2,1)} %pad_maximum_fusion.1.refs_0_.refs_31_, bf16[384,512]{1,0:T(8,128)(2,1)} %bitcast.87, ...), custom_call_target="tpu_custom_call" | custom-call | flops 2415919104 | bytes 10381312 | tf_op jit(solution)/shard_map/stem/pallas_call | solution.py:150
  75.4 1.1 copy-done.2
  76.5 4.8 project.2
  81.2 5.8 %attend.3 = (bf16[448,512]{1,0:T(8,128)(2,1)}, f32[32,448]{1,0:T(8,128)}) custom-call(bf16[448,1536]{1,0:T(8,128)(2,1)} %get-tuple-element.85.query_ref.key_ref.value_ref, bf16[448,1536]{1,0:T(8,128)(2,1)} %get-tuple-element.85.query_ref.key_ref.value_ref, bf16[448,1536]{1,0:T(8,128)(2,1)} %get-tuple-element.85.query_ref.key_ref.value_ref), custom_call_target="tpu_custom_call" | custom-call | flops 1644167168 | bytes 1835008 | tf_op jit(solution)/shard_map/attend/pallas_call | solution.py:260
  87.1 73.1 %collective-permute-done.2.refs_3_.refs_7_.refs_15_ = bf16[1,512,512]{2,1,0:T(8,128)(2,1)S(1)} collective-permute-done((bf16[1,512,512]{2,1,0:T(8,128)(2,1)S(1)}, bf16[1,512,512]{2,1,0:T(8,128)(2,1)S(1)}, u32[]{:S(2)}, u32[]{:S(2)}) %collective-permute-start.2) | collective-permute-done | bytes 524320 | tf_op jit(solution)/shard_map/ppermute | solution.py:1027
  160.2 11.2 %collective-permute-done.3.refs_6_.refs_11_.refs_5_.refs_7_ = bf16[1,512,512]{2,1,0:T(8,128)(2,1)S(1)} collective-permute-done((bf16[1,512,512]{2,1,0:T(8,128)(2,1)S(1)}, bf16[1,512,512]{2,1,0:T(8,128)(2,1)S(1)}, u32[]{:S(2)}, u32[]{:S(2)}) %collective-permute-start.3) | collective-permute-done | bytes 524320 | tf_op jit(solution)/shard_map/ppermute | solution.py:1027
  172.3 4.5 text_middle.1
  176.7 7.2 %project.3 = (bf16[1024,512]{1,0:T(8,128)(2,1)}, bf16[1024,1536]{1,0:T(8,128)(2,1)}) custom-call(f32[1024,512]{1,0:T(8,128)} %get-tuple-element.89.refs_0_.refs_3_, bf16[1,512,1536]{2,1,0:T(8,128)(2,1)} %refs_6_.9, bf16[1,512,1536]{2,1,0:T(8,128)(2,1)} %copy-done.2, f32[12,512]{1,0:T(8,128)} %bitcast.99), custom_call_target="tpu_custom_call" | custom-call | flops 1610612736 | bytes 9461760 | tf_op jit(solution)/shard_map/project/pallas_call | solution.py:150
  183.9 21.2 %attend.4 = (bf16[1024,512]{1,0:T(8,128)(2,1)}, f32[32,1024]{1,0:T(8,128)}) custom-call(bf16[1024,1536]{1,0:T(8,128)(2,1)} %get-tuple-element.90.query_ref.key_ref.value_ref, bf16[1024,1536]{1,0:T(8,128)(2,1)} %get-tuple-element.90.query_ref.key_ref.value_ref, bf16[1024,1536]{1,0:T(8,128)(2,1)} %get-tuple-element.90.query_ref.key_ref.value_ref), custom_call_target="tpu_custom_call" | custom-call | flops 8589934592 | bytes 4194304 | tf_op jit(solution)/shard_map/attend/pallas_call | solution.py:260
  206.7 20.5 %audio_feed.1 = (f32[1024,512]{1,0:T(8,128)}, bf16[1024,512]{1,0:T(8,128)(2,1)}, bf16[1024,2048]{1,0:T(8,128)(2,1)}, bf16[1024,2048]{1,0:T(8,128)(2,1)}, f32[102...) custom-call(f32[1024,512]{1,0:T(8,128)} %get-tuple-element.89.refs_0_.refs_3_, ...), custom_call_target="tpu_custom_call" | custom-call | flops 5905580032 | bytes 29392896 | tf_op jit(solution)/shard_map/audio_feed/pallas_call | solution.py:150
  227.2 9.4 %attend.5 = (bf16[448,512]{1,0:T(8,128)(2,1)}, f32[32,448]{1,0:T(8,128)}) custom-call(bf16[448,512]{1,0:T(8,128)(2,1)} %get-tuple-element.88.query_ref, bf16[1024,512]{1,0:T(8,128)(2,1)} %get-tuple-element.92.key_ref, bf16[1024,512]{1,0:T(8,128)(2,1)} %get-tuple-element.93.value_ref), custom_call_target="tpu_custom_call" | custom-call | flops 3758096384 | bytes 3014656 | tf_op jit(solution)/shard_map/attend/pallas_call | solution.py:260
  236.5 15.4 %text_feed.1 = (f32[448,512]{1,0:T(8,128)}, bf16[448,512]{1,0:T(8,128)(2,1)}, bf16[448,2048]{1,0:T(8,128)(2,1)}, bf16[448,2048]{1,0:T(8,128)(2,1)}, bf16[448,512...) custom-call(s32[1]{0:T(128)} %dynamic_slice.27.refs_0_, ...), custom_call_target="tpu_custom_call" | custom-call | flops 4227858432 | bytes 17768452 | tf_op jit(solution)/shard_map/text_feed/pallas_call | solution.py:150
  251.9 1.9 select_convert_fusion.2
  253.8 1.2 select_bitcast_fusion.2
  255.0 14.0 %attend_back.3 = (bf16[448,512]{1,0:T(8,128)(2,1)}, bf16[1024,512]{1,0:T(8,128)(2,1)}, bf16[1024,512]{1,0:T(8,128)(2,1)}, f32[8,512]{1,0:T(8,128)}) custom-call(bf16[448,512]{1,0:T(8,128)(2,1)} %get-tuple-element.88.query_ref, bf16[1024,512]{1,0:T(8,128)(2,1)} %get-tuple-element.92.key_ref, bf16[1024,512]{1,0:T(8,128)(2,1)} %get-tuple-element.93.value_ref, ...), custom_call_target="tpu_custom_call" | custom-call | flops 9395240960 | bytes 6029312 | tf_op jit(solution)/shard_map/attend_back/pallas_call | solution.py:337
  269.0 4.8 text_cross_back.1
  273.9 8.2 %attend_back.4 = (bf16[448,512]{1,0:T(8,128)(2,1)}, bf16[448,512]{1,0:T(8,128)(2,1)}, bf16[448,512]{1,0:T(8,128)(2,1)}, f32[8,512]{1,0:T(8,128)}) custom-call(bf16[448,1536]{1,0:T(8,128)(2,1)} %get-tuple-element.85.query_ref.key_ref.value_ref, bf16[448,1536]{1,0:T(8,128)(2,1)} %get-tuple-element.85.query_ref.key_ref.value_ref, ...), custom_call_target="tpu_custom_call" | custom-call | flops 4110417920 | bytes 3670016 | tf_op jit(solution)/shard_map/attend_back/pallas_call | solution.py:337
  282.1 5.4 project_back.1
  287.5 1.9 select_convert_fusion.1
  289.4 1.2 select_bitcast_fusion.1
  290.6 15.7 %audio_feed_back.1 = (bf16[1024,512]{1,0:T(8,128)(2,1)}, bf16[1024,2048]{1,0:T(8,128)(2,1)}, f32[1024,512]{1,0:T(8,128)}, bf16[1024,512]{1,0:T(8,128)(2,1)}, bf1...) custom-call(bf16[1024,512]{1,0:T(8,128)(2,1)} %get-tuple-element.108.refs_0_.refs_11_, ...), custom_call_target="tpu_custom_call" | custom-call | flops 5905580032 | bytes 30474240 | tf_op jit(solution)/shard_map/audio_feed_back/pallas_call | solution.py:150
  306.4 34.4 %attend_back.5 = (bf16[1024,512]{1,0:T(8,128)(2,1)}, bf16[1024,512]{1,0:T(8,128)(2,1)}, bf16[1024,512]{1,0:T(8,128)(2,1)}, f32[8,512]{1,0:T(8,128)}) custom-call(bf16[1024,1536]{1,0:T(8,128)(2,1)} %get-tuple-element.90.query_ref.key_ref.value_ref, bf16[1024,1536]{1,0:T(8,128)(2,1)} %get-tuple-element.90.query_ref.key_ref.value_ref, ...), custom_call_target="tpu_custom_call" | custom-call | flops 21474836480 | bytes 8388608 | tf_op jit(solution)/shard_map/attend_back/pallas_call | solution.py:337
  340.7 11.8 %stem_back.1 = (bf16[1024,512]{1,0:T(8,128)(2,1)}, bf16[1024,512]{1,0:T(8,128)(2,1)}, bf16[1024,512]{1,0:T(8,128)(2,1)}, bf16[1024,512]{1,0:T(8,128)(2,1)}, f32[1024,512]{1,0:T(8,128)}, /*index=5*/f32[8,512]{1,0:T(8,128)}) custom-call(bf16[1024,512]{1,0:T(8,128)(2,1)} %get-tuple-element.114.refs_0_.refs_1_, ...), custom_call_target="tpu_custom_call" | custom-call | flops 4026531840 | bytes 20873216 | tf_op jit(solution)/shard_map/stem_back/pallas_call | solution.py:150
  352.5 1.3 fusion.11
  353.8 1.3 add_bitcast_fusion.1
  356.6 0.9 fusion.4
  357.5 0.9 fusion.5
  360.8 41.9 %weight_grads.1.flat_ref = bf16[2,8192,512]{2,1,0:T(8,128)(2,1)} custom-call(bf16[1024,512]{1,0:T(8,128)(2,1)} %get-tuple-element.122.refs_0_, bf16[1024,512]{1,0:T(8,128)(2,1)} %get-tuple-element.114.refs_0_.refs_1_, bf16[1024,512]{1,0:T(8,128)(2,1)} %get-tuple-element.115.refs_1_.refs_2_, bf16[1024,512]{1,0:T(8,128)(2,1)} %get-tuple-element.116.refs_2_.refs_3_, ...), custom_call_target="tpu_custom_call" | custom-call | flops 13488881664 | bytes 36503552 | tf_op jit(solution)/shard_map/weight_grads/pallas_call | solution.py:762
  402.7 123.7 %reduce_all.1 = bf16[8192,512]{1,0:T(8,128)(2,1)} custom-call(bf16[2,8192,512]{2,1,0:T(8,128)(2,1)} %weight_grads.1.flat_ref), custom_call_target="tpu_custom_call" | custom-call | bytes 838860800 | tf_op jit(solution)/shard_map/reduce_all/pallas_call | solution.py:966
  526.3 1.0 fusion.10
  527.3 1.3 fusion.7
  528.5 1.2 fusion.9
  529.8 11.6 %convert_element_type.52 = f32[8192,512]{1,0:T(8,128)} convert(bf16[8192,512]{1,0:T(8,128)(2,1)} %reduce_all.1) | non-fusion elementwise | flops 4194304 | bytes 25165824 | tf_op jit(solution)/shard_map/convert_element_type | solution.py:1147
  541.4 2.7 fusion.8
  544.9 3.6 slice_bitcast_fusion.1
  548.5 4.6 slice_bitcast_fusion
  555.9 1.5 collective-permute-start.10
  557.9 1.3 collective-permute-start.12
  559.2 1.2 pad_maximum_fusion
  560.5 1.9 maximum_bitcast_fusion.1
  562.3 2.4 maximum_bitcast_fusion
  567.9 6.5 %collective-permute-done.12 = bf16[512]{0:T(512)(128)(2,1)S(1)} collective-permute-done((bf16[512]{0:T(512)(128)(2,1)S(1)}, bf16[512]{0:T(512)(128)(2,1)S(1)}, u32[]{:S(2)}, u32[]{:S(2)}) %collective-permute-start.12) | collective-permute-done | bytes 1056 | tf_op jit(solution)/shard_map/ppermute | solution.py:1169
  575.1 1.2 copy.45
  576.3 1.0 bitcast_convert_fusion.2
  577.2 1.0 maximum_select_fusion.2
  578.2 1.0 bitcast_convert_fusion.1
  579.2 1.0 maximum_select_fusion.3
  (119 shorter events, 22.8 us)
Async XLA Ops:
  0.7 21.6 %copy-start = (bf16[2,448,512]{2,1,0:T(8,128)(2,1)S(1)}, bf16[2,448,512]{2,1,0:T(8,128)(2,1)}, u32[]{:S(2)}) copy-start(bf16[2,448,512]{2,1,0:T(8,128)(2,1)} %param.28) | copy-start | bytes 2752516
  0.7 74.6 %collective-permute-start = (bf16[1,512,1536]{2,1,0:T(8,128)(2,1)}, bf16[1,512,1536]{2,1,0:T(8,128)(2,1)S(1)}, u32[]{:S(2)}, u32[]{:S(2)}) collective-permute-start(bf16[1,512,1536]{2,1,0:T(8,128)(2,1)} %refs_6_.9), channel_id=1, source_target_pairs={{0,16},{16,0},{1,17},{17,1},{2,18},{18,2},{3,19},{19,3},{4,20},{20... | collective-permute-start | bytes 4718600 | tf_op jit(solution)/shard_map/ppermute | solution.py:1027
  5.2 34.3 %collective-permute-start.1 = (bf16[16,512]{1,0:T(8,128)(2,1)S(1)}, bf16[16,512]{1,0:T(8,128)(2,1)S(1)}, u32[]{:S(2)}, u32[]{:S(2)}) collective-permute-start(bf16[16,512]{1,0:T(8,128)(2,1)S(1)} %pad_maximum_fusion.5), channel_id=1, source_target_pairs={{0,16},{16,0},{1,17},{17,1},{2,18},{18,2},{3,19},{19,3},{4,20},{20... | collective-permute-start | bytes 49160 | tf_op jit(solution)/shard_map/ppermute | solution.py:1027
  7.5 35.3 %collective-permute-start.4 = (bf16[241,256]{1,0:T(8,128)(2,1)}, bf16[241,256]{1,0:T(8,128)(2,1)S(1)}, u32[]{:S(2)}, u32[]{:S(2)}) collective-permute-start(bf16[241,256]{1,0:T(8,128)(2,1)} %pad_maximum_fusion.4), channel_id=1, source_target_pairs={{0,16},{16,0},{1,17},{17,1},{2,18},{18,2},{3,19},{19,3},{4,20},{20... | collective-permute-start | bytes 370184 | tf_op jit(solution)/shard_map/ppermute | solution.py:1027
  9.5 49.7 %collective-permute-start.5 = (bf16[3,512,256]{2,1,0:T(8,128)(2,1)}, bf16[3,512,256]{2,1,0:T(8,128)(2,1)}, u32[]{:S(2)}, u32[]{:S(2)}) collective-permute-start(bf16[3,512,256]{2,1,0:T(8,128)(2,1)} %param.33), channel_id=1, source_target_pairs={{0,16},{16,0},{1,17},{17,1},{2,18},{18,2},{3,19},{19,3},{4,20},{20... | collective-permute-start | bytes 2359304 | tf_op jit(solution)/shard_map/ppermute | solution.py:1027
  9.6 195.6 %collective-permute-start.6 = (bf16[1,512,2048]{2,1,0:T(8,128)(2,1)}, bf16[1,512,2048]{2,1,0:T(8,128)(2,1)}, u32[]{:S(2)}, u32[]{:S(2)}) collective-permute-start(bf16[1,512,2048]{2,1,0:T(8,128)(2,1)} %refs_10_.5), channel_id=1, source_target_pairs={{0,16},{16,0},{1,17},{17,1},{2,18},{18,2},{3,19},{19,3},{4,20},{20... | collective-permute-start | bytes 6291464 | tf_op jit(solution)/shard_map/ppermute | solution.py:1027
  22.0 2.4 copy-start.13
  22.1 3.1 copy-start.23
  22.1 19.4 %copy-start.14 = (bf16[1,6,512]{2,1,0:T(8,128)(2,1)S(1)}, bf16[1,6,512]{2,1,0:T(8,128)(2,1)}, u32[]{:S(2)}) copy-start(bf16[1,6,512]{2,1,0:T(8,128)(2,1)} %param.41) | copy-start | bytes 18436
  22.1 19.4 %copy-start.15 = (bf16[1,3,512]{2,1,0:T(4,128)(2,1)S(1)}, bf16[1,3,512]{2,1,0:T(4,128)(2,1)}, u32[]{:S(2)}) copy-start(bf16[1,3,512]{2,1,0:T(4,128)(2,1)} %param.35) | copy-start | bytes 9220
  22.2 19.4 %copy-start.16 = (bf16[1,3,512]{2,1,0:T(4,128)(2,1)S(1)}, bf16[1,3,512]{2,1,0:T(4,128)(2,1)}, u32[]{:S(2)}) copy-start(bf16[1,3,512]{2,1,0:T(4,128)(2,1)} %param.34) | copy-start | bytes 9220
  22.2 20.7 %copy-start.3 = (bf16[1,512,512]{2,1,0:T(8,128)(2,1)S(1)}, bf16[1,512,512]{2,1,0:T(8,128)(2,1)}, u32[]{:S(2)}) copy-start(bf16[1,512,512]{2,1,0:T(8,128)(2,1)} %refs_14_.1) | copy-start | bytes 1572868
  22.2 22.1 %copy-start.11 = (bf16[3,80,256]{2,1,0:T(8,128)(2,1)S(1)}, bf16[3,80,256]{2,1,0:T(8,128)(2,1)}, u32[]{:S(2)}) copy-start(bf16[3,80,256]{2,1,0:T(8,128)(2,1)} %param.31) | copy-start | bytes 368644
  23.1 36.0 %copy-start.4 = (bf16[1,512,512]{2,1,0:T(8,128)(2,1)S(1)}, bf16[1,512,512]{2,1,0:T(8,128)(2,1)}, u32[]{:S(2)}) copy-start(bf16[1,512,512]{2,1,0:T(8,128)(2,1)} %refs_6_.8) | copy-start | bytes 1572868
  39.5 165.7 %collective-permute-start.7 = (bf16[1,2048,512]{2,1,0:T(8,128)(2,1)}, bf16[1,2048,512]{2,1,0:T(8,128)(2,1)S(1)}, u32[]{:S(2)}, u32[]{:S(2)}) collective-permute-start(bf16[1,2048,512]{2,1,0:T(8,128)(2,1)} %refs_12_.3), channel_id=1, source_target_pairs={{0,16},{16,0},{1,17},{17,1},{2,18},{18,2},{3,19},{19,3},{4,20},{20... | collective-permute-start | bytes 6291464 | tf_op jit(solution)/shard_map/ppermute | solution.py:1027
  41.6 23.1 %copy-start.12 = (f32[16,512]{1,0:T(8,128)}, f32[16,512]{1,0:T(8,128)S(1)}, u32[]{:S(2)}) copy-start(f32[16,512]{1,0:T(8,128)S(1)} %get-tuple-element.211) | copy-start | bytes 98308
  41.6 33.7 %copy-start.8 = (f32[16,512]{1,0:T(8,128)}, f32[16,512]{1,0:T(8,128)S(1)}, u32[]{:S(2)}) copy-start(f32[16,512]{1,0:T(8,128)S(1)} %get-tuple-element.212) | copy-start | bytes 98308
  42.8 117.3 %collective-permute-start.2 = (bf16[1,512,512]{2,1,0:T(8,128)(2,1)S(1)}, bf16[1,512,512]{2,1,0:T(8,128)(2,1)S(1)}, u32[]{:S(2)}, u32[]{:S(2)}) collective-permute-start(bf16[1,512,512]{2,1,0:T(8,128)(2,1)S(1)} %copy-done.3), channel_id=1, source_target_pairs={{0,16},{16,0},{1,17},{17,1},{2,18},{18,2},{3,19},{19,3},{4,20},{20... | collective-permute-start | bytes 1572872 | tf_op jit(solution)/shard_map/ppermute | solution.py:1027
  59.2 112.2 %collective-permute-start.3 = (bf16[1,512,512]{2,1,0:T(8,128)(2,1)S(1)}, bf16[1,512,512]{2,1,0:T(8,128)(2,1)S(1)}, u32[]{:S(2)}, u32[]{:S(2)}) collective-permute-start(bf16[1,512,512]{2,1,0:T(8,128)(2,1)S(1)} %copy-done.4), channel_id=1, source_target_pairs={{0,16},{16,0},{1,17},{17,1},{2,18},{18,2},{3,19},{19,3},{4,20},{20... | collective-permute-start | bytes 1572872 | tf_op jit(solution)/shard_map/ppermute | solution.py:1027
  64.7 10.6 %copy-start.9 = (bf16[1,512,512]{2,1,0:T(8,128)(2,1)S(1)}, bf16[1,512,512]{2,1,0:T(8,128)(2,1)}, u32[]{:S(2)}) copy-start(bf16[1,512,512]{2,1,0:T(8,128)(2,1)} %refs_8_.5) | copy-start | bytes 1572868
  75.3 1.1 copy-start.2
  75.3 129.8 %collective-permute-start.8 = (bf16[1,512,512]{2,1,0:T(8,128)(2,1)S(1)}, bf16[1,512,512]{2,1,0:T(8,128)(2,1)S(1)}, u32[]{:S(2)}, u32[]{:S(2)}) collective-permute-start(bf16[1,512,512]{2,1,0:T(8,128)(2,1)S(1)} %copy-done.9), channel_id=1, source_target_pairs={{0,16},{16,0},{1,17},{17,1},{2,18},{18,2},{3,19},{19,3},{4,20},{20... | collective-permute-start | bytes 1572872 | tf_op jit(solution)/shard_map/ppermute | solution.py:1027
  160.2 11.2 %copy-start.5 = (bf16[1,512,512]{2,1,0:T(8,128)(2,1)}, bf16[1,512,512]{2,1,0:T(8,128)(2,1)S(1)}, u32[]{:S(2)}) copy-start(bf16[1,512,512]{2,1,0:T(8,128)(2,1)S(1)} %collective-permute-done.2.refs_3_.refs_7_.refs_15_) | copy-start | bytes 1572868
  171.4 0.8 copy-start.6
  205.2 0.8 copy-start.10
  205.2 1.5 copy-start.7
  355.2 1.3 copy-start.22
  355.2 3.1 copy-start.21
  355.2 3.2 copy-start.19
  355.2 3.2 copy-start.17
  355.2 4.0 copy-start.18
  355.2 4.0 copy-start.20
  555.3 20.9 %collective-permute-start.9 = (bf16[448,256]{1,0:T(8,128)(2,1)}, bf16[448,256]{1,0:T(8,128)(2,1)}, u32[]{:S(2)}, u32[]{:S(2)}) collective-permute-start(bf16[448,256]{1,0:T(8,128)(2,1)} %select_convert_fusion.2), channel_id=1, source_target_pairs={{0,16},{16,0},{1,17},{17,1},{2,18},{18,2},{3,19},{19,3},{4,20},{20... | collective-permute-start | bytes 688136 | tf_op jit(solution)/shard_map/ppermute | solution.py:1027
  555.9 22.3 %collective-permute-start.10 = (bf16[448,256]{1,0:T(8,128)(2,1)}, bf16[448,256]{1,0:T(8,128)(2,1)}, u32[]{:S(2)}, u32[]{:S(2)}) collective-permute-start(bf16[448,256]{1,0:T(8,128)(2,1)} %select_convert_fusion.1), channel_id=1, source_target_pairs={{0,16},{16,0},{1,17},{17,1},{2,18},{18,2},{3,19},{19,3},{4,20},{20... | collective-permute-start | bytes 688136 | tf_op jit(solution)/shard_map/ppermute | solution.py:1027
  557.4 17.6 %collective-permute-start.11 = (bf16[80,1024]{0,1:T(8,128)(2,1)S(1)}, bf16[80,1024]{0,1:T(8,128)(2,1)S(1)}, u32[]{:S(2)}, u32[]{:S(2)}) collective-permute-start(bf16[80,1024]{0,1:T(8,128)(2,1)S(1)} %select_convert_fusion), channel_id=1, source_target_pairs={{0,16},{16,0},{1,17},{17,1},{2,18},{18,2},{3,19},{19,3},{4,20},{20... | collective-permute-start | bytes 491528 | tf_op jit(solution)/shard_map/ppermute | solution.py:1027
  557.9 16.5 %collective-permute-start.12 = (bf16[512]{0:T(512)(128)(2,1)S(1)}, bf16[512]{0:T(512)(128)(2,1)S(1)}, u32[]{:S(2)}, u32[]{:S(2)}) collective-permute-start(bf16[512]{0:T(512)(128)(2,1)S(1)} %slice_reduce_fusion), channel_id=1, source_target_pairs={{16,0},{17,1},{18,2},{19,3},{20,4},{21,5},{22,6},{23,7},{24,8},{25... | collective-permute-start | bytes 3080 | tf_op jit(solution)/shard_map/ppermute | solution.py:1169
  575.0 5.2 copy-start.1
